TPU v7x, 32 devices: a whole 2x2x4 slice. The times are simulated.
32 devices in a mesh: space: 8 (over z, x), tm: 4 (over y, core).
Axes of the slice: x: 2, y: 2, z: 4, core: 2. Of those that a mesh axis runs over, the one named last changes fastest.
Arguments:
- field: bfloat16 [1024, 196608], P('tm', 'space'), may hold values from -6 to 6
- temporal_cov: bfloat16 [1024, 1024], replicated
- spatial_blocks: bfloat16 [1536, 9, 128, 128], P(('space', 'tm')), may hold values from -0.3125 to 0.3125
- neighbours: int32 [1536, 9], P(('space', 'tm')), may hold values from -4 to 1539, as said below
- counts: int32 [1536], P(('space', 'tm')), may hold values from 1 to 9, as said below
Outputs:
- covariant_field: bfloat16 [1024, 196608], P('tm', 'space')
Inputs may be any that keep to these rules, and one draw needn't show every extreme that they name: `neighbours`: row b holds b + o for every o from -4 to 4, each once, in an order drawn for each row; values outside 0 to 1535 name blocks of zeros. counts[b] is the number of leading slots of row b that are used.
All inputs are finite; a program needn't handle non-finite values.
Results may differ from a plain program's by a relative error of at most 0.005.
Values may be sent and summed in bfloat16 or wider, within the bound.
No kernel may reach another device: no remote copies, remote signals or barrier semaphores. Data moves between devices by JAX's collectives and lax.ppermute only.
A program may use at most 512 MiB of HBM per device.

v0:
```python
import functools

import jax
import jax.numpy as jnp
from jax import lax
from jax.experimental import pallas as pl
from jax.experimental.pallas import tpu as pltpu
from jax.sharding import PartitionSpec as P


CHUNK_UNITS = 3
MiB = 1 << 20


def ascends(group):
    return jnp.bitwise_and(group, 1) == 1


def pack_kernel(last, sources, place_ref, *refs):
    inputs, targets = refs[: -len(sources)], refs[-len(sources) :]
    low_ref, high_ref = inputs[len(sources) :] if len(inputs) > len(sources) else (None, None)
    for peer, target in enumerate(targets):
        value = inputs[peer][...]
        if low_ref is not None:
            at = sources[peer](pl.program_id(0), place_ref)
            value = jnp.where(at < 0, low_ref[...], jnp.where(at > last, high_ref[...], value))
        target[...] = value


def pack(field, place, halo, peers, unit, group_units, first, count, groups):
    hours_dev = field.shape[0]
    last = groups * group_units - 1

    def source_of(peer):
        def source(i, place):
            group = place[peer]
            start = jnp.where(ascends(group), first, group_units - first - count)
            return group * group_units + start + i

        return source

    sources = [source_of(peer) for peer in peers]

    def spec(source):
        return pl.BlockSpec(
            (hours_dev, unit), lambda i, place: (0, jnp.clip(source(i, place), 0, last))
        )

    in_specs = [spec(source) for source in sources]
    operands = [field] * len(peers)
    if halo is not None:
        in_specs += [pl.BlockSpec((hours_dev, unit), lambda i, place: (0, 0))] * 2
        operands += list(halo)
    return pl.pallas_call(
        functools.partial(pack_kernel, last, sources),
        out_shape=[jax.ShapeDtypeStruct((hours_dev, count * unit), field.dtype) for _ in peers],
        grid_spec=pltpu.PrefetchScalarGridSpec(
            num_scalar_prefetch=1,
            grid=(count,),
            in_specs=in_specs,
            out_specs=[pl.BlockSpec((hours_dev, unit), lambda i, place: (0, i)) for _ in peers],
        ),
        cost_estimate=pl.CostEstimate(
            flops=0,
            transcendentals=0,
            bytes_accessed=4 * len(peers) * hours_dev * count * unit,
        ),
        name="pack",
    )(place, *operands)


def rows_kernel(place_ref, source, target):
    target[...] = source[...]


def order_rows(temporal_cov, place, groups):
    hours_all = temporal_cov.shape[0]
    hours_dev = hours_all // groups
    return pl.pallas_call(
        rows_kernel,
        out_shape=jax.ShapeDtypeStruct(temporal_cov.shape, temporal_cov.dtype),
        grid_spec=pltpu.PrefetchScalarGridSpec(
            num_scalar_prefetch=1,
            grid=(groups,),
            in_specs=[pl.BlockSpec((hours_dev, hours_all), lambda i, place: (place[i], 0))],
            out_specs=pl.BlockSpec((hours_dev, hours_all), lambda i, place: (i, 0)),
        ),
        name="order",
    )(place, temporal_cov)


def product_kernel(cfg, place_ref, neighbours_ref, counts_ref, cov_ref, *refs):
    groups, unit, block, slots, chunk_units, group_units, first_out, lead = cfg["dims"]
    opening, has_next = cfg["flags"]
    refs = list(refs)
    pieces = [refs.pop(0) for _ in range(groups)]
    inner = [refs.pop(0) for _ in range(groups)] if opening else None
    outset = [refs.pop(0) for _ in range(groups)] if opening else None
    carry_ref = None if opening else refs.pop(0)
    tiles_ref = refs.pop(0)
    outs = [refs.pop(0) for _ in range(groups)]
    next_ref = refs.pop(0) if has_next else None
    panel, mixed, banded = refs

    step = pl.program_id(0)
    steps = pl.num_programs(0)
    upward = ascends(place_ref[0])
    hours_dev = pieces[0].shape[0]
    reach = (slots - 1) // 2
    width = slots + 1

    def columns(position):
        at = jnp.where(upward, position, chunk_units + 1 - position)
        return pl.ds(pl.multiple_of(at * unit, unit), unit)

    @pl.when(step == 0)
    def _():
        for pair in range(banded.shape[0]):
            banded[pair, :block, slots * block :] = jnp.zeros((block, block), banded.dtype)
            banded[pair, block:, :block] = jnp.zeros((block, block), banded.dtype)
        if not opening:
            for which in range(2):
                mixed[:, columns(which)] = carry_ref[:, which * unit : (which + 1) * unit]

    def load(sources):
        for peer in range(groups):
            at = pl.multiple_of(place_ref[peer] * hours_dev, hours_dev)
            panel[pl.ds(at, hours_dev), :] = sources[peer][...]

    if opening:
        pl.when(step == 0)(lambda: load(inner))
        pl.when(step == 1)(lambda: load(outset))
        pl.when(step >= 2)(lambda: load(pieces))
    else:
        load(pieces)

    fresh = jnp.dot(cov_ref[...], panel[...], preferred_element_type=jnp.float32).astype(mixed.dtype)
    mixed[:, columns(step + lead)] = fresh
    if has_next:
        for which in range(2):

            @pl.when(step == steps - 2 + which)
            def _():
                next_ref[:, which * unit : (which + 1) * unit] = fresh

    @pl.when(step + lead >= 2)
    def _():
        turn = step + lead - 2
        at = jnp.where(upward, turn, chunk_units - 1 - turn)
        own_unit = jnp.where(upward, first_out + turn, group_units - 1 - first_out - turn)
        first_row = own_unit * (unit // block)
        base = pl.multiple_of(at * unit, unit)
        for pair in range(unit // block // 2):
            for which in range(2):
                row = 2 * pair + which
                mine = first_row + row
                block_id = place_ref[groups] + mine
                live = counts_ref[mine]
                for slot in range(slots):
                    offset = neighbours_ref[mine, slot] - block_id + (reach + which)
                    offset = jnp.clip(offset, 0, slots)
                    tile = tiles_ref[row, slot]
                    banded[
                        pair,
                        which * block : (which + 1) * block,
                        pl.ds(pl.multiple_of(offset * block, block), block),
                    ] = jnp.where(slot < live, tile, jnp.zeros_like(tile))
            window = mixed[:, pl.ds(pl.multiple_of(base + 2 * pair * block, block), width * block)]
            summed = lax.dot_general(
                window, banded[pair], (((1,), (1,)), ((), ())), preferred_element_type=jnp.float32
            ).astype(outs[0].dtype)
            for peer in range(groups):
                outs[peer][:, 2 * pair * block : 2 * (pair + 1) * block] = summed[
                    peer * hours_dev : (peer + 1) * hours_dev
                ]


def products(place, neighbours, counts, cov, pieces, start, carry, spatial_blocks, layout, chunk):
    groups, unit, block, slots, group_units, chunk_units = layout
    chunks = group_units // chunk_units
    hours_all, hours_dev = cov.shape[0], pieces[0].shape[0]
    opening, has_next = chunk == 0, chunk < chunks - 1
    lead = 0 if opening else 2
    steps = chunk_units + 2 - lead
    first_out = chunk * chunk_units

    def piece_index(i, place, *_):
        turn = jnp.maximum(i + lead - 2, 0)
        return 0, jnp.where(ascends(place[0]), turn, chunk_units - 1 - turn)

    def tile_index(i, place, *_):
        turn = first_out + jnp.maximum(i + lead - 2, 0)
        return jnp.where(ascends(place[0]), turn, group_units - 1 - turn), 0, 0, 0

    def whole(shape):
        return pl.BlockSpec(shape, lambda i, *_: (0, 0))

    piece_spec = pl.BlockSpec((hours_dev, unit), piece_index)
    in_specs = [whole((hours_all, hours_all))] + [piece_spec] * groups
    operands = [cov] + list(pieces)
    if opening:
        in_specs += [whole((hours_dev, unit))] * (2 * groups)
        operands += list(start[0]) + list(start[1])
    else:
        in_specs += [whole((hours_all, 2 * unit))]
        operands += [carry]
    blocks_unit = unit // block
    in_specs += [pl.BlockSpec((blocks_unit, slots, block, block), tile_index)]
    operands += [spatial_blocks]
    dtype = pieces[0].dtype
    out_shape = [jax.ShapeDtypeStruct((hours_dev, chunk_units * unit), dtype)] * groups
    out_specs = [piece_spec] * groups
    if has_next:
        out_shape += [jax.ShapeDtypeStruct((hours_all, 2 * unit), dtype)]
        out_specs += [whole((hours_all, 2 * unit))]
    cfg = {
        "dims": (groups, unit, block, slots, chunk_units, group_units, first_out, lead),
        "flags": (opening, has_next),
    }
    flops = 2 * hours_all * unit * (steps * hours_all + chunk_units * (slots + 1) * block)
    results = pl.pallas_call(
        functools.partial(product_kernel, cfg),
        out_shape=out_shape,
        grid_spec=pltpu.PrefetchScalarGridSpec(
            num_scalar_prefetch=3,
            grid=(steps,),
            in_specs=in_specs,
            out_specs=out_specs,
            scratch_shapes=[
                pltpu.VMEM((hours_all, unit), dtype),
                pltpu.VMEM((hours_all, (chunk_units + 2) * unit), dtype),
                pltpu.VMEM((blocks_unit // 2, 2 * block, (slots + 1) * block), dtype),
            ],
        ),
        compiler_params=pltpu.CompilerParams(vmem_limit_bytes=48 * MiB),
        cost_estimate=pl.CostEstimate(
            flops=flops,
            transcendentals=0,
            bytes_accessed=2 * hours_all * unit * (steps + chunk_units)
            + 2 * chunk_units * blocks_unit * slots * block * block,
        ),
        name="products",
    )(place, neighbours, counts, *operands)
    return results[:groups], (results[groups] if has_next else None)


def place_kernel(peers, chunks, chunk, place_ref, *refs):
    target, sems = refs[-2], refs[-1]
    copies = []
    for which, peer in enumerate(peers):
        source = refs[which]
        columns = source.shape[1]
        group = place_ref[peer]
        at = group * chunks + jnp.where(ascends(group), chunk, chunks - 1 - chunk)
        copies.append(
            pltpu.make_async_copy(
                source,
                target.at[:, pl.ds(pl.multiple_of(at * columns, columns), columns)],
                sems.at[which],
            )
        )
    for copy in copies:
        copy.start()
    for copy in copies:
        copy.wait()


def put(result, pieces, peers, place, cells_dev, chunks, chunk):
    hours_dev, columns = pieces[0].shape
    in_specs = [pl.BlockSpec(memory_space=pltpu.VMEM)] * len(pieces)
    operands = list(pieces)
    aliases = {}
    if result is not None:
        in_specs += [pl.BlockSpec(memory_space=pl.ANY)]
        operands += [result]
        aliases = {1 + len(pieces): 0}
    return pl.pallas_call(
        functools.partial(place_kernel, peers, chunks, chunk),
        out_shape=jax.ShapeDtypeStruct((hours_dev, cells_dev), pieces[0].dtype),
        grid_spec=pltpu.PrefetchScalarGridSpec(
            num_scalar_prefetch=1,
            grid=(),
            in_specs=in_specs,
            out_specs=pl.BlockSpec(memory_space=pl.ANY),
            scratch_shapes=[pltpu.SemaphoreType.DMA((len(pieces),))],
        ),
        input_output_aliases=aliases,
        cost_estimate=pl.CostEstimate(
            flops=0, transcendentals=0, bytes_accessed=4 * len(pieces) * hours_dev * columns
        ),
        name="place",
    )(place, *operands)


def per_device(field, temporal_cov, spatial_blocks, neighbours, counts):
    groups = lax.axis_size("tm")
    spaces = lax.axis_size("space")
    _, cells_dev = field.shape
    per_group, slots, block = spatial_blocks.shape[:3]
    reach = (slots - 1) // 2
    unit = reach * block
    group_units = per_group // reach
    chunk_units = CHUNK_UNITS if group_units % CHUNK_UNITS == 0 else group_units
    chunks = group_units // chunk_units
    layout = (groups, unit, block, slots, group_units, chunk_units)

    mine = lax.axis_index("tm")
    first_block = (lax.axis_index("space") * groups + mine) * per_group
    place = jnp.concatenate(
        [
            jnp.bitwise_xor(mine.astype(jnp.int32), jnp.arange(groups, dtype=jnp.int32)),
            first_block.astype(jnp.int32)[None],
        ]
    )

    def swap(array, peer):
        return lax.ppermute(array, "tm", [(at, at ^ peer) for at in range(groups)])

    def swap_all(arrays):
        moved = {peer: swap(arrays[peer], peer) for peer in range(groups - 1, 0, -1)}
        return [arrays[0]] + [moved[peer] for peer in range(1, groups)]

    forward = [(at, at + 1) for at in range(spaces - 1)]
    backward = [(to, at) for at, to in forward]
    peers = list(range(groups))

    first_sent = pack(field, place, None, peers, unit, group_units, 0, 1, groups)
    first = swap_all(first_sent)
    low = lax.ppermute(field[:, cells_dev - unit :], "space", forward)
    high = lax.ppermute(field[:, :unit], "space", backward)
    arrived, sent = [], first_sent
    for chunk in range(chunks):
        halo = (low, high) if chunk == chunks - 1 else None
        turn, _ = lax.optimization_barrier((place, sent[-1]))
        sent = pack(
            field, turn, halo, peers, unit, group_units,
            1 + chunk * chunk_units, chunk_units, groups,
        )
        arrived.append(swap_all(sent))
    inner = [first_sent[1]] + [swap(first[peer ^ 1], 1) for peer in range(1, groups)]
    cov = order_rows(temporal_cov, place, groups)
    carry, result = None, None
    returned = []
    for chunk in range(chunks):
        outs, carry = products(
            place, neighbours, counts, cov, arrived[chunk], (inner, first), carry,
            spatial_blocks, layout, chunk,
        )
        returned.append(swap_all(outs))
    for chunk in range(chunks):
        near, far = (peers, []) if chunk < chunks - 1 else (peers[:2], peers[2:])
        for listed in (near, far):
            if listed:
                result = put(
                    result, [returned[chunk][peer] for peer in listed], listed, place,
                    cells_dev, chunks, chunk,
                )
    return result


def solution(mesh):
    placed = (
        P("tm", "space"),
        P(),
        P(("space", "tm"), None, None, None),
        P(("space", "tm"), None),
        P(("space", "tm")),
    )
    return jax.shard_map(
        per_device, mesh=mesh, in_specs=placed, out_specs=P("tm", "space"), check_vma=False
    )
```

profile of v0, /device:TPU:16, one launch (start us, length us, event | category | flops | bytes accessed | tf_op | source)
XLA Modules:
  0.0 299.9 jit_solution(7098779692035533554)
XLA Ops:
  0.7 2.8 pack.5
  3.5 1.0 collective-permute-start.15
  5.5 1.1 fusion
  6.6 3.4 %collective-permute-start = (bf16[256,512]{1,0:T(8,128)(2,1)S(1)}, bf16[256,512]{1,0:T(8,128)(2,1)S(1)}, u32[]{:S(2)}, u32[]{:S(2)}) collective-permute-start(bf16[256,512]{1,0:T(8,128)(2,1)S(1)} %get-tuple-element.92), channel_id=1, source_target_pairs={{0,4},{4,8},{8,12},{12,16},{16,20},{20,24},{24,28},{1,5},{5,9},{9,... | collective-permute-start | bytes 786440 | tf_op jit(solution)/shard_map/ppermute | solution.py:329
  10.0 5.1 %pack.6 = (bf16[256,1536]{1,0:T(8,128)(2,1)}, bf16[256,1536]{1,0:T(8,128)(2,1)}, bf16[256,1536]{1,0:T(8,128)(2,1)}, bf16[256,1536]{1,0:T(8,128)(2,1)}) custom-call(s32[5]{0:T(128)} %pad_add_fusion.place_ref, bf16[256,24576]{1,0:T(8,128)(2,1)} %refs_3_.9, bf16[256,24576]{1,0:T(8,128)(2,1)} %refs_3_.9, bf16[256,24576]{1,0:T(8,128)(2,1)} %refs_3_.9, ...), custom_call_target="tpu_custom_call" | custom-call | bytes 6291456 | tf_op jit(solution)/shard_map/pack/pallas_call | solution.py:54
  15.1 3.3 %collective-permute-start.1 = (bf16[256,512]{1,0:T(8,128)(2,1)S(1)}, bf16[256,512]{1,0:T(8,128)(2,1)S(1)}, u32[]{:S(2)}, u32[]{:S(2)}) collective-permute-start(bf16[256,512]{1,0:T(8,128)(2,1)S(1)} %get-tuple-element.91), channel_id=1, source_target_pairs={{4,0},{8,4},{12,8},{16,12},{20,16},{24,20},{28,24},{5,1},{9,5},{13... | collective-permute-start | bytes 786440 | tf_op jit(solution)/shard_map/ppermute | solution.py:330
  18.5 5.1 %pack.7 = (bf16[256,1536]{1,0:T(8,128)(2,1)}, bf16[256,1536]{1,0:T(8,128)(2,1)}, bf16[256,1536]{1,0:T(8,128)(2,1)}, bf16[256,1536]{1,0:T(8,128)(2,1)}) custom-call(s32[5]{0:T(128)} %pad_add_fusion.place_ref, bf16[256,24576]{1,0:T(8,128)(2,1)} %refs_3_.9, bf16[256,24576]{1,0:T(8,128)(2,1)} %refs_3_.9, bf16[256,24576]{1,0:T(8,128)(2,1)} %refs_3_.9, ...), custom_call_target="tpu_custom_call" | custom-call | bytes 6291456 | tf_op jit(solution)/shard_map/pack/pallas_call | solution.py:54
  23.5 1.0 collective-permute-start.13
  25.8 0.9 collective-permute-start.10
  26.6 0.7 collective-permute-start.16
  27.4 1.2 collective-permute-done.16.refs_6_
  28.9 4.5 %order.1.cov_ref = bf16[1024,1024]{1,0:T(8,128)(2,1)} custom-call(s32[5]{0:T(128)} %pad_add_fusion.place_ref, bf16[1024,1024]{1,0:T(8,128)(2,1)} %source.1), custom_call_target="tpu_custom_call" | custom-call | tf_op jit(solution)/shard_map/order/pallas_call | solution.py:79
  33.4 5.1 %pack.8 = (bf16[256,1536]{1,0:T(8,128)(2,1)}, bf16[256,1536]{1,0:T(8,128)(2,1)}, bf16[256,1536]{1,0:T(8,128)(2,1)}, bf16[256,1536]{1,0:T(8,128)(2,1)}) custom-call(s32[5]{0:T(128)} %pad_add_fusion.place_ref, bf16[256,24576]{1,0:T(8,128)(2,1)} %refs_3_.9, bf16[256,24576]{1,0:T(8,128)(2,1)} %refs_3_.9, bf16[256,24576]{1,0:T(8,128)(2,1)} %refs_3_.9, ...), custom_call_target="tpu_custom_call" | custom-call | bytes 6291456 | tf_op jit(solution)/shard_map/pack/pallas_call | solution.py:54
  38.6 5.3 %pack.9 = (bf16[256,1536]{1,0:T(8,128)(2,1)}, bf16[256,1536]{1,0:T(8,128)(2,1)}, bf16[256,1536]{1,0:T(8,128)(2,1)}, bf16[256,1536]{1,0:T(8,128)(2,1)}) custom-call(s32[5]{0:T(128)} %pad_add_fusion.place_ref, bf16[256,24576]{1,0:T(8,128)(2,1)} %refs_3_.9, bf16[256,24576]{1,0:T(8,128)(2,1)} %refs_3_.9, bf16[256,24576]{1,0:T(8,128)(2,1)} %refs_3_.9, ...), custom_call_target="tpu_custom_call" | custom-call | bytes 6291456 | tf_op jit(solution)/shard_map/pack/pallas_call | solution.py:54
  45.3 1.4 collective-permute-start.9
  46.8 13.9 %collective-permute-done.12.refs_2_ = bf16[256,1536]{1,0:T(8,128)(2,1)} collective-permute-done((bf16[256,1536]{1,0:T(8,128)(2,1)}, bf16[256,1536]{1,0:T(8,128)(2,1)}, u32[]{:S(2)}, u32[]{:S(2)}) %collective-permute-start.12) | collective-permute-done | bytes 786464 | tf_op jit(solution)/shard_map/ppermute | solution.py:317
  60.7 16.7 %collective-permute-done.10.refs_3_ = bf16[256,1536]{1,0:T(8,128)(2,1)} collective-permute-done((bf16[256,1536]{1,0:T(8,128)(2,1)}, bf16[256,1536]{1,0:T(8,128)(2,1)}, u32[]{:S(2)}, u32[]{:S(2)}) %collective-permute-start.10) | collective-permute-done | bytes 786464 | tf_op jit(solution)/shard_map/ppermute | solution.py:317
  77.5 1.5 collective-permute-start.6
  79.0 0.9 copy-done.12
  79.9 17.9 %products.4 = (bf16[256,1536]{1,0:T(8,128)(2,1)S(1)}, bf16[256,1536]{1,0:T(8,128)(2,1)S(1)}, bf16[256,1536]{1,0:T(8,128)(2,1)S(1)}, bf16[256,1536]{1,0:T(8,128)(2,1)S(1)}, bf16[1024,1024]{1,0:T(8,128)(2,1)}) custom-call(s32[5]{0:T(128)S(1)} %copy-done.4, s32[48,9]{1,0:T(8,128)S(1)} %copy.13.neighbours_ref, s32[48]{0:T(128)S(1)} %copy-done.13, ...), custom_call_target="tpu_custom_call" | custom-call | flops 9395240960 | bytes 11927552 | tf_op jit(solution)/shard_map/products/pallas_call | solution.py:221
  97.9 0.9 copy-done
  98.8 12.3 %collective-permute-done.9.refs_2_ = bf16[256,1536]{1,0:T(8,128)(2,1)S(1)} collective-permute-done((bf16[256,1536]{1,0:T(8,128)(2,1)}, bf16[256,1536]{1,0:T(8,128)(2,1)S(1)}, u32[]{:S(2)}, u32[]{:S(2)}) %collective-permute-start.9) | collective-permute-done | bytes 786464 | tf_op jit(solution)/shard_map/ppermute | solution.py:317
  111.1 1.5 collective-permute-start.3
  113.3 14.6 %collective-permute-done.6.refs_2_ = bf16[256,1536]{1,0:T(8,128)(2,1)S(1)} collective-permute-done((bf16[256,1536]{1,0:T(8,128)(2,1)}, bf16[256,1536]{1,0:T(8,128)(2,1)S(1)}, u32[]{:S(2)}, u32[]{:S(2)}) %collective-permute-start.6) | collective-permute-done | bytes 786464 | tf_op jit(solution)/shard_map/ppermute | solution.py:317
  127.9 1.5 collective-permute-start.30
  129.4 15.6 %products.5 = (bf16[256,1536]{1,0:T(8,128)(2,1)S(1)}, bf16[256,1536]{1,0:T(8,128)(2,1)S(1)}, bf16[256,1536]{1,0:T(8,128)(2,1)S(1)}, bf16[256,1536]{1,0:T(8,128)(2,1)S(1)}, bf16[1024,1024]{1,0:T(8,128)(2,1)}) custom-call(s32[5]{0:T(128)S(1)} %copy-done.4, s32[48,9]{1,0:T(8,128)S(1)} %copy.13.neighbours_ref, s32[48]{0:T(128)S(1)} %copy-done.13, ...), custom_call_target="tpu_custom_call" | custom-call | flops 7247757312 | bytes 9830400 | tf_op jit(solution)/shard_map/products/pallas_call | solution.py:221
  145.0 0.9 copy-done.3
  145.9 15.5 %products.6 = (bf16[256,1536]{1,0:T(8,128)(2,1)S(1)}, bf16[256,1536]{1,0:T(8,128)(2,1)S(1)}, bf16[256,1536]{1,0:T(8,128)(2,1)S(1)}, bf16[256,1536]{1,0:T(8,128)(2,1)S(1)}, bf16[1024,1024]{1,0:T(8,128)(2,1)}) custom-call(s32[5]{0:T(128)S(1)} %copy-done.4, s32[48,9]{1,0:T(8,128)S(1)} %copy.13.neighbours_ref, s32[48]{0:T(128)S(1)} %copy-done.13, ...), custom_call_target="tpu_custom_call" | custom-call | flops 7247757312 | bytes 9830400 | tf_op jit(solution)/shard_map/products/pallas_call | solution.py:221
  161.4 0.9 copy-done.2
  163.0 1.5 collective-permute-start.27
  164.5 14.0 %collective-permute-done.30.refs_2_ = bf16[256,1536]{1,0:T(8,128)(2,1)S(1)} collective-permute-done((bf16[256,1536]{1,0:T(8,128)(2,1)S(1)}, bf16[256,1536]{1,0:T(8,128)(2,1)S(1)}, u32[]{:S(2)}, u32[]{:S(2)}) %collective-permute-start.30) | collective-permute-done | bytes 786464 | tf_op jit(solution)/shard_map/ppermute | solution.py:317
  178.6 0.8 copy-done.15
  179.4 14.9 %products.7 = (bf16[256,1536]{1,0:T(8,128)(2,1)S(1)}, bf16[256,1536]{1,0:T(8,128)(2,1)}, bf16[256,1536]{1,0:T(8,128)(2,1)S(1)}, bf16[256,1536]{1,0:T(8,128)(2,1)S(1)}) custom-call(s32[5]{0:T(128)S(1)} %copy-done.4, s32[48,9]{1,0:T(8,128)S(1)} %copy.13.neighbours_ref, s32[48]{0:T(128)S(1)} %copy-done.13, bf16[1024,1024]{1,0:T(8,128)(2,1)} %order.1.cov_ref, ...), custom_call_target="tpu_custom_call" | custom-call | flops 7247757312 | bytes 9830400 | tf_op jit(solution)/shard_map/products/pallas_call | solution.py:221
  194.3 0.9 copy-done.1
  195.3 1.5 collective-permute-start.24
  196.8 15.4 %collective-permute-done.27.refs_2_ = bf16[256,1536]{1,0:T(8,128)(2,1)S(1)} collective-permute-done((bf16[256,1536]{1,0:T(8,128)(2,1)S(1)}, bf16[256,1536]{1,0:T(8,128)(2,1)S(1)}, u32[]{:S(2)}, u32[]{:S(2)}) %collective-permute-start.27) | collective-permute-done | bytes 786464 | tf_op jit(solution)/shard_map/ppermute | solution.py:317
  212.3 16.7 %collective-permute-done.28.refs_3_ = bf16[256,1536]{1,0:T(8,128)(2,1)S(1)} collective-permute-done((bf16[256,1536]{1,0:T(8,128)(2,1)S(1)}, bf16[256,1536]{1,0:T(8,128)(2,1)S(1)}, u32[]{:S(2)}, u32[]{:S(2)}) %collective-permute-start.28) | collective-permute-done | bytes 786464 | tf_op jit(solution)/shard_map/ppermute | solution.py:317
  229.0 1.5 collective-permute-start.20
  230.5 0.8 copy-done.19
  231.4 4.2 %place.5.refs_4_ = bf16[256,24576]{1,0:T(8,128)(2,1)} custom-call(s32[5]{0:T(128)} %pad_add_fusion.place_ref, bf16[256,1536]{1,0:T(8,128)(2,1)} %copy-done, bf16[256,1536]{1,0:T(8,128)(2,1)} %copy-done.14, bf16[256,1536]{1,0:T(8,128)(2,1)} %copy-done.15, bf16[256,1536]{1,0:T(8,128)(2,1)} %copy-done.16), custom_call_target="tpu_custom_call" | custom-call | bytes 6291456 | tf_op jit(solution)/shard_map/place/pallas_call | solution.py:277
  235.6 4.2 %place.6.refs_4_ = bf16[256,24576]{1,0:T(8,128)(2,1)} custom-call(s32[5]{0:T(128)} %pad_add_fusion.place_ref, bf16[256,1536]{1,0:T(8,128)(2,1)} %copy-done.3, bf16[256,1536]{1,0:T(8,128)(2,1)} %copy-done.17, bf16[256,1536]{1,0:T(8,128)(2,1)} %copy-done.18, bf16[256,1536]{1,0:T(8,128)(2,1)} %copy-done.20, ...), custom_call_target="tpu_custom_call", output_to_operand_aliasing={{}: (5, {})} | custom-call | bytes 6291456 | tf_op jit(solution)/shard_map/place/pallas_call | solution.py:277
  239.8 6.2 %collective-permute-done.24.refs_2_ = bf16[256,1536]{1,0:T(8,128)(2,1)} collective-permute-done((bf16[256,1536]{1,0:T(8,128)(2,1)S(1)}, bf16[256,1536]{1,0:T(8,128)(2,1)}, u32[]{:S(2)}, u32[]{:S(2)}) %collective-permute-start.24) | collective-permute-done | bytes 786464 | tf_op jit(solution)/shard_map/ppermute | solution.py:317
  246.0 16.8 %collective-permute-done.25.refs_3_ = bf16[256,1536]{1,0:T(8,128)(2,1)} collective-permute-done((bf16[256,1536]{1,0:T(8,128)(2,1)S(1)}, bf16[256,1536]{1,0:T(8,128)(2,1)}, u32[]{:S(2)}, u32[]{:S(2)}) %collective-permute-start.25) | collective-permute-done | bytes 786464 | tf_op jit(solution)/shard_map/ppermute | solution.py:317
  262.8 4.2 %place.7.refs_2_ = bf16[256,24576]{1,0:T(8,128)(2,1)} custom-call(s32[5]{0:T(128)} %pad_add_fusion.place_ref, bf16[256,1536]{1,0:T(8,128)(2,1)} %copy-done.2, bf16[256,1536]{1,0:T(8,128)(2,1)} %copy-done.19, bf16[256,1536]{1,0:T(8,128)(2,1)} %collective-permute-done.24.refs_2_, ...), custom_call_target="tpu_custom_call", output_to_operand_aliasing={{}: (5, {})} | custom-call | bytes 6291456 | tf_op jit(solution)/shard_map/place/pallas_call | solution.py:277
  267.1 3.2 %place.8.refs_2_ = bf16[256,24576]{1,0:T(8,128)(2,1)} custom-call(s32[5]{0:T(128)} %pad_add_fusion.place_ref, bf16[256,1536]{1,0:T(8,128)(2,1)} %copy-done.1, bf16[256,1536]{1,0:T(8,128)(2,1)} %collective-permute-done.22.refs_1_, bf16[256,24576]{1,0:T(8,128)(2,1)} %place.7.refs_2_), custom_call_target="tpu_custom_call", output_to_operand_aliasing={{}: (3, {})} | custom-call | bytes 3145728 | tf_op jit(solution)/shard_map/place/pallas_call | solution.py:277
  270.2 9.5 %collective-permute-done.20.refs_0_ = bf16[256,1536]{1,0:T(8,128)(2,1)} collective-permute-done((bf16[256,1536]{1,0:T(8,128)(2,1)S(1)}, bf16[256,1536]{1,0:T(8,128)(2,1)}, u32[]{:S(2)}, u32[]{:S(2)}) %collective-permute-start.20) | collective-permute-done | bytes 786464 | tf_op jit(solution)/shard_map/ppermute | solution.py:317
  279.7 16.8 %collective-permute-done.21.refs_1_ = bf16[256,1536]{1,0:T(8,128)(2,1)} collective-permute-done((bf16[256,1536]{1,0:T(8,128)(2,1)S(1)}, bf16[256,1536]{1,0:T(8,128)(2,1)}, u32[]{:S(2)}, u32[]{:S(2)}) %collective-permute-start.21) | collective-permute-done | bytes 786464 | tf_op jit(solution)/shard_map/ppermute | solution.py:317
  296.5 3.2 %place.9 = bf16[256,24576]{1,0:T(8,128)(2,1)} custom-call(s32[5]{0:T(128)} %pad_add_fusion.place_ref, bf16[256,1536]{1,0:T(8,128)(2,1)} %collective-permute-done.20.refs_0_, bf16[256,1536]{1,0:T(8,128)(2,1)} %collective-permute-done.21.refs_1_, bf16[256,24576]{1,0:T(8,128)(2,1)} %place.8.refs_2_), custom_call_target="tpu_custom_call", output_to_operand_aliasing={{}: (3, {})} | custom-call | bytes 3145728 | tf_op jit(solution)/shard_map/place/pallas_call | solution.py:277
  (87 shorter events, 6.7 us)
Async XLA Ops:
  3.5 11.6 %collective-permute-start.15 = (bf16[256,512]{1,0:T(8,128)(2,1)}, bf16[256,512]{1,0:T(8,128)(2,1)S(1)}, u32[]{:S(2)}, u32[]{:S(2)}) collective-permute-start(bf16[256,512]{1,0:T(8,128)(2,1)} %get-tuple-element.48), channel_id=1, source_target_pairs={{0,3},{1,2},{2,1},{3,0},{4,7},{5,6},{6,5},{7,4},{8,11},{9,10},{10,... | collective-permute-start | bytes 786440 | tf_op jit(solution)/shard_map/ppermute | solution.py:317
  4.4 19.1 %collective-permute-start.17 = (bf16[256,512]{1,0:T(8,128)(2,1)}, bf16[256,512]{1,0:T(8,128)(2,1)S(1)}, u32[]{:S(2)}, u32[]{:S(2)}) collective-permute-start(bf16[256,512]{1,0:T(8,128)(2,1)} %get-tuple-element.71), channel_id=1, source_target_pairs={{0,2},{1,3},{2,0},{3,1},{4,6},{5,7},{6,4},{7,5},{8,10},{9,11},{10,... | collective-permute-start | bytes 786440 | tf_op jit(solution)/shard_map/ppermute | solution.py:317
  5.0 19.5 %collective-permute-start.14 = (bf16[256,512]{1,0:T(8,128)(2,1)}, bf16[256,512]{1,0:T(8,128)(2,1)S(1)}, u32[]{:S(2)}, u32[]{:S(2)}) collective-permute-start(bf16[256,512]{1,0:T(8,128)(2,1)} %get-tuple-element.70.refs_8_), channel_id=1, source_target_pairs={{0,1},{1,0},{2,3},{3,2},{4,5},{5,4},{6,7},{7,6},{8,9},{9,8},{10,11... | collective-permute-start | bytes 786440 | tf_op jit(solution)/shard_map/ppermute | solution.py:317
  5.4 19.8 %collective-permute-start.19 = (bf16[256,512]{1,0:T(8,128)(2,1)}, bf16[256,512]{1,0:T(8,128)(2,1)S(1)}, u32[]{:S(2)}, u32[]{:S(2)}) collective-permute-start(bf16[256,512]{1,0:T(8,128)(2,1)} %get-tuple-element.69.refs_4_), channel_id=1, source_target_pairs={{0,1},{1,0},{2,3},{3,2},{4,5},{5,4},{6,7},{7,6},{8,9},{9,8},{10,11... | collective-permute-start | bytes 786440 | tf_op jit(solution)/shard_map/ppermute | solution.py:317
  6.6 19.2 %collective-permute-start = (bf16[256,512]{1,0:T(8,128)(2,1)S(1)}, bf16[256,512]{1,0:T(8,128)(2,1)S(1)}, u32[]{:S(2)}, u32[]{:S(2)}) collective-permute-start(bf16[256,512]{1,0:T(8,128)(2,1)S(1)} %get-tuple-element.92), channel_id=1, source_target_pairs={{0,4},{4,8},{8,12},{12,16},{16,20},{20,24},{24,28},{1,5},{5,9},{9,... | collective-permute-start | bytes 786440 | tf_op jit(solution)/shard_map/ppermute | solution.py:329
  15.1 18.3 %copy-start.23 = (s32[48,9]{0,1:T(8,128)S(1)}, s32[48,9]{0,1:T(8,128)}, u32[]{:S(2)}) copy-start(s32[48,9]{0,1:T(8,128)} %param.8) | copy-start | bytes 5188
  15.1 11.5 %collective-permute-start.1 = (bf16[256,512]{1,0:T(8,128)(2,1)S(1)}, bf16[256,512]{1,0:T(8,128)(2,1)S(1)}, u32[]{:S(2)}, u32[]{:S(2)}) collective-permute-start(bf16[256,512]{1,0:T(8,128)(2,1)S(1)} %get-tuple-element.91), channel_id=1, source_target_pairs={{4,0},{8,4},{12,8},{16,12},{20,16},{24,20},{28,24},{5,1},{9,5},{13... | collective-permute-start | bytes 786440 | tf_op jit(solution)/shard_map/ppermute | solution.py:330
  23.5 21.4 %collective-permute-start.13 = (bf16[256,1536]{1,0:T(8,128)(2,1)}, bf16[256,1536]{1,0:T(8,128)(2,1)}, u32[]{:S(2)}, u32[]{:S(2)}) collective-permute-start(bf16[256,1536]{1,0:T(8,128)(2,1)} %get-tuple-element.50), channel_id=1, source_target_pairs={{0,3},{1,2},{2,1},{3,0},{4,7},{5,6},{6,5},{7,4},{8,11},{9,10},{10,... | collective-permute-start | bytes 2359304 | tf_op jit(solution)/shard_map/ppermute | solution.py:317
  24.5 20.8 %collective-permute-start.11 = (bf16[256,1536]{1,0:T(8,128)(2,1)}, bf16[256,1536]{1,0:T(8,128)(2,1)}, u32[]{:S(2)}, u32[]{:S(2)}) collective-permute-start(bf16[256,1536]{1,0:T(8,128)(2,1)} %get-tuple-element.67), channel_id=1, source_target_pairs={{0,1},{1,0},{2,3},{3,2},{4,5},{5,4},{6,7},{7,6},{8,9},{9,8},{10,11... | collective-permute-start | bytes 2359304 | tf_op jit(solution)/shard_map/ppermute | solution.py:317
  25.2 35.4 %collective-permute-start.12 = (bf16[256,1536]{1,0:T(8,128)(2,1)}, bf16[256,1536]{1,0:T(8,128)(2,1)}, u32[]{:S(2)}, u32[]{:S(2)}) collective-permute-start(bf16[256,1536]{1,0:T(8,128)(2,1)} %get-tuple-element.68), channel_id=1, source_target_pairs={{0,2},{1,3},{2,0},{3,1},{4,6},{5,7},{6,4},{7,5},{8,10},{9,11},{10,... | collective-permute-start | bytes 2359304 | tf_op jit(solution)/shard_map/ppermute | solution.py:317
  25.8 12.8 %copy-start.21 = (bf16[256,512]{1,0:T(8,128)(2,1)}, bf16[256,512]{1,0:T(8,128)(2,1)S(1)}, u32[]{:S(2)}) copy-start(bf16[256,512]{1,0:T(8,128)(2,1)S(1)} %collective-permute-done.refs_4_) | copy-start | bytes 786436
  25.8 51.7 %collective-permute-start.10 = (bf16[256,1536]{1,0:T(8,128)(2,1)}, bf16[256,1536]{1,0:T(8,128)(2,1)}, u32[]{:S(2)}, u32[]{:S(2)}) collective-permute-start(bf16[256,1536]{1,0:T(8,128)(2,1)} %get-tuple-element.52), channel_id=1, source_target_pairs={{0,3},{1,2},{2,1},{3,0},{4,7},{5,6},{6,5},{7,4},{8,11},{9,10},{10,... | collective-permute-start | bytes 2359304 | tf_op jit(solution)/shard_map/ppermute | solution.py:317
  26.6 1.9 collective-permute-start.16
  28.5 15.4 %collective-permute-start.18 = (bf16[256,512]{1,0:T(8,128)(2,1)S(1)}, bf16[256,512]{1,0:T(8,128)(2,1)S(1)}, u32[]{:S(2)}, u32[]{:S(2)}) collective-permute-start(bf16[256,512]{1,0:T(8,128)(2,1)S(1)} %collective-permute-done.17.refs_10_), channel_id=1, source_target_pairs={{0,1},{1,0},{2,3},{3,2},{4,5},{5,4},{6,7},{7,6},{8,9},{9,8},{10,11... | collective-permute-start | bytes 786440 | tf_op jit(solution)/shard_map/ppermute | solution.py:317
  38.5 40.4 %copy-start.4 = (s32[5]{0:T(128)S(1)}, s32[5]{0:T(128)}, u32[]{:S(2)}) copy-start(s32[5]{0:T(128)} %pad_add_fusion.place_ref) | copy-start | bytes 64
  38.5 40.4 %copy-start.7 = (bf16[256,1536]{1,0:T(8,128)(2,1)S(1)}, bf16[256,1536]{1,0:T(8,128)(2,1)}, u32[]{:S(2)}) copy-start(bf16[256,1536]{1,0:T(8,128)(2,1)} %get-tuple-element.66.refs_0_) | copy-start | bytes 2359300
  38.6 40.4 %copy-start.9 = (bf16[256,512]{1,0:T(8,128)(2,1)S(1)}, bf16[256,512]{1,0:T(8,128)(2,1)}, u32[]{:S(2)}) copy-start(bf16[256,512]{1,0:T(8,128)(2,1)} %get-tuple-element.70.refs_8_) | copy-start | bytes 786436
  38.6 40.4 %copy-start.10 = (bf16[256,512]{1,0:T(8,128)(2,1)S(1)}, bf16[256,512]{1,0:T(8,128)(2,1)}, u32[]{:S(2)}) copy-start(bf16[256,512]{1,0:T(8,128)(2,1)} %get-tuple-element.69.refs_4_) | copy-start | bytes 786436
  38.6 40.4 %copy-start.13 = (s32[48]{0:T(128)S(1)}, s32[48]{0:T(128)}, u32[]{:S(2)}) copy-start(s32[48]{0:T(128)} %counts_ref.7) | copy-start | bytes 580
  44.6 67.9 %collective-permute-start.7 = (bf16[256,1536]{1,0:T(8,128)(2,1)}, bf16[256,1536]{1,0:T(8,128)(2,1)S(1)}, u32[]{:S(2)}, u32[]{:S(2)}) collective-permute-start(bf16[256,1536]{1,0:T(8,128)(2,1)} %get-tuple-element.54), channel_id=1, source_target_pairs={{0,3},{1,2},{2,1},{3,0},{4,7},{5,6},{6,5},{7,4},{8,11},{9,10},{10,... | collective-permute-start | bytes 2359304 | tf_op jit(solution)/shard_map/ppermute | solution.py:317
  44.9 53.8 %collective-permute-start.8 = (bf16[256,1536]{1,0:T(8,128)(2,1)}, bf16[256,1536]{1,0:T(8,128)(2,1)S(1)}, u32[]{:S(2)}, u32[]{:S(2)}) collective-permute-start(bf16[256,1536]{1,0:T(8,128)(2,1)} %get-tuple-element.64), channel_id=1, source_target_pairs={{0,1},{1,0},{2,3},{3,2},{4,5},{5,4},{6,7},{7,6},{8,9},{9,8},{10,11... | collective-permute-start | bytes 2359304 | tf_op jit(solution)/shard_map/ppermute | solution.py:317
  45.3 65.8 %collective-permute-start.9 = (bf16[256,1536]{1,0:T(8,128)(2,1)}, bf16[256,1536]{1,0:T(8,128)(2,1)S(1)}, u32[]{:S(2)}, u32[]{:S(2)}) collective-permute-start(bf16[256,1536]{1,0:T(8,128)(2,1)} %get-tuple-element.65), channel_id=1, source_target_pairs={{0,2},{1,3},{2,0},{3,1},{4,6},{5,7},{6,4},{7,5},{8,10},{9,11},{10,... | collective-permute-start | bytes 2359304 | tf_op jit(solution)/shard_map/ppermute | solution.py:317
  60.6 52.0 %collective-permute-start.5 = (bf16[256,1536]{1,0:T(8,128)(2,1)}, bf16[256,1536]{1,0:T(8,128)(2,1)S(1)}, u32[]{:S(2)}, u32[]{:S(2)}) collective-permute-start(bf16[256,1536]{1,0:T(8,128)(2,1)} %get-tuple-element.61), channel_id=1, source_target_pairs={{0,1},{1,0},{2,3},{3,2},{4,5},{5,4},{6,7},{7,6},{8,9},{9,8},{10,11... | collective-permute-start | bytes 2359304 | tf_op jit(solution)/shard_map/ppermute | solution.py:317
  77.5 50.5 %collective-permute-start.6 = (bf16[256,1536]{1,0:T(8,128)(2,1)}, bf16[256,1536]{1,0:T(8,128)(2,1)S(1)}, u32[]{:S(2)}, u32[]{:S(2)}) collective-permute-start(bf16[256,1536]{1,0:T(8,128)(2,1)} %get-tuple-element.62), channel_id=1, source_target_pairs={{0,2},{1,3},{2,0},{3,1},{4,6},{5,7},{6,4},{7,5},{8,10},{9,11},{10,... | collective-permute-start | bytes 2359304 | tf_op jit(solution)/shard_map/ppermute | solution.py:317
  79.9 32.7 %copy-start.24 = (bf16[256,1536]{1,0:T(8,128)(2,1)S(1)}, bf16[256,1536]{1,0:T(8,128)(2,1)}, u32[]{:S(2)}) copy-start(bf16[256,1536]{1,0:T(8,128)(2,1)} %get-tuple-element.59) | copy-start | bytes 2359300
  79.9 49.5 %copy-start.6 = (bf16[256,1536]{1,0:T(8,128)(2,1)S(1)}, bf16[256,1536]{1,0:T(8,128)(2,1)}, u32[]{:S(2)}) copy-start(bf16[256,1536]{1,0:T(8,128)(2,1)} %get-tuple-element.63.refs_0_) | copy-start | bytes 2359300
  98.7 63.6 %collective-permute-start.2 = (bf16[256,1536]{1,0:T(8,128)(2,1)}, bf16[256,1536]{1,0:T(8,128)(2,1)S(1)}, u32[]{:S(2)}, u32[]{:S(2)}) collective-permute-start(bf16[256,1536]{1,0:T(8,128)(2,1)} %get-tuple-element.57), channel_id=1, source_target_pairs={{0,1},{1,0},{2,3},{3,2},{4,5},{5,4},{6,7},{7,6},{8,9},{9,8},{10,11... | collective-permute-start | bytes 2359304 | tf_op jit(solution)/shard_map/ppermute | solution.py:317
  111.1 51.2 %collective-permute-start.3 = (bf16[256,1536]{1,0:T(8,128)(2,1)}, bf16[256,1536]{1,0:T(8,128)(2,1)S(1)}, u32[]{:S(2)}, u32[]{:S(2)}) collective-permute-start(bf16[256,1536]{1,0:T(8,128)(2,1)} %get-tuple-element.58), channel_id=1, source_target_pairs={{0,2},{1,3},{2,0},{3,1},{4,6},{5,7},{6,4},{7,5},{8,10},{9,11},{10,... | collective-permute-start | bytes 2359304 | tf_op jit(solution)/shard_map/ppermute | solution.py:317
  112.6 32.4 %copy-start.25 = (bf16[256,1536]{1,0:T(8,128)(2,1)}, bf16[256,1536]{1,0:T(8,128)(2,1)S(1)}, u32[]{:S(2)}) copy-start(bf16[256,1536]{1,0:T(8,128)(2,1)S(1)} %collective-permute-done.7.refs_3_) | copy-start | bytes 2359300
  112.6 50.4 %collective-permute-start.4 = (bf16[256,1536]{1,0:T(8,128)(2,1)S(1)}, bf16[256,1536]{1,0:T(8,128)(2,1)}, u32[]{:S(2)}, u32[]{:S(2)}) collective-permute-start(bf16[256,1536]{1,0:T(8,128)(2,1)S(1)} %copy-done.24), channel_id=1, source_target_pairs={{0,3},{1,2},{2,1},{3,0},{4,7},{5,6},{6,5},{7,4},{8,11},{9,10},{10,... | collective-permute-start | bytes 2359304 | tf_op jit(solution)/shard_map/ppermute | solution.py:317
  112.6 51.8 %collective-permute-start.29 = (bf16[256,1536]{1,0:T(8,128)(2,1)S(1)}, bf16[256,1536]{1,0:T(8,128)(2,1)S(1)}, u32[]{:S(2)}, u32[]{:S(2)}) collective-permute-start(bf16[256,1536]{1,0:T(8,128)(2,1)S(1)} %get-tuple-element.88), channel_id=1, source_target_pairs={{0,1},{1,0},{2,3},{3,2},{4,5},{5,4},{6,7},{7,6},{8,9},{9,8},{10,11... | collective-permute-start | bytes 2359304 | tf_op jit(solution)/shard_map/ppermute | solution.py:317
  127.9 50.6 %collective-permute-start.30 = (bf16[256,1536]{1,0:T(8,128)(2,1)S(1)}, bf16[256,1536]{1,0:T(8,128)(2,1)S(1)}, u32[]{:S(2)}, u32[]{:S(2)}) collective-permute-start(bf16[256,1536]{1,0:T(8,128)(2,1)S(1)} %get-tuple-element.89), channel_id=1, source_target_pairs={{0,2},{1,3},{2,0},{3,1},{4,6},{5,7},{6,4},{7,5},{8,10},{9,11},{10,... | collective-permute-start | bytes 2359304 | tf_op jit(solution)/shard_map/ppermute | solution.py:317
  129.4 16.5 %copy-start.8 = (bf16[256,1536]{1,0:T(8,128)(2,1)S(1)}, bf16[256,1536]{1,0:T(8,128)(2,1)}, u32[]{:S(2)}) copy-start(bf16[256,1536]{1,0:T(8,128)(2,1)} %get-tuple-element.60.refs_0_) | copy-start | bytes 2359300
  145.9 33.5 %copy-start.5 = (bf16[256,1536]{1,0:T(8,128)(2,1)S(1)}, bf16[256,1536]{1,0:T(8,128)(2,1)}, u32[]{:S(2)}) copy-start(bf16[256,1536]{1,0:T(8,128)(2,1)} %get-tuple-element.56.refs_0_) | copy-start | bytes 2359300
  162.3 33.0 %collective-permute-start.31 = (bf16[256,1536]{1,0:T(8,128)(2,1)S(1)}, bf16[256,1536]{1,0:T(8,128)(2,1)S(1)}, u32[]{:S(2)}, u32[]{:S(2)}) collective-permute-start(bf16[256,1536]{1,0:T(8,128)(2,1)S(1)} %get-tuple-element.90), channel_id=1, source_target_pairs={{0,3},{1,2},{2,1},{3,0},{4,7},{5,6},{6,5},{7,4},{8,11},{9,10},{10,... | collective-permute-start | bytes 2359304 | tf_op jit(solution)/shard_map/ppermute | solution.py:317
  162.3 34.5 %collective-permute-start.26 = (bf16[256,1536]{1,0:T(8,128)(2,1)S(1)}, bf16[256,1536]{1,0:T(8,128)(2,1)S(1)}, u32[]{:S(2)}, u32[]{:S(2)}) collective-permute-start(bf16[256,1536]{1,0:T(8,128)(2,1)S(1)} %get-tuple-element.84), channel_id=1, source_target_pairs={{0,1},{1,0},{2,3},{3,2},{4,5},{5,4},{6,7},{7,6},{8,9},{9,8},{10,11... | collective-permute-start | bytes 2359304 | tf_op jit(solution)/shard_map/ppermute | solution.py:317
  163.0 49.2 %collective-permute-start.27 = (bf16[256,1536]{1,0:T(8,128)(2,1)S(1)}, bf16[256,1536]{1,0:T(8,128)(2,1)S(1)}, u32[]{:S(2)}, u32[]{:S(2)}) collective-permute-start(bf16[256,1536]{1,0:T(8,128)(2,1)S(1)} %get-tuple-element.85), channel_id=1, source_target_pairs={{0,2},{1,3},{2,0},{3,1},{4,6},{5,7},{6,4},{7,5},{8,10},{9,11},{10,... | collective-permute-start | bytes 2359304 | tf_op jit(solution)/shard_map/ppermute | solution.py:317
  164.5 29.8 %copy-start.14 = (bf16[256,1536]{1,0:T(8,128)(2,1)}, bf16[256,1536]{1,0:T(8,128)(2,1)S(1)}, u32[]{:S(2)}) copy-start(bf16[256,1536]{1,0:T(8,128)(2,1)S(1)} %collective-permute-done.29.refs_1_) | copy-start | bytes 2359300
  164.5 64.6 %collective-permute-start.28 = (bf16[256,1536]{1,0:T(8,128)(2,1)S(1)}, bf16[256,1536]{1,0:T(8,128)(2,1)S(1)}, u32[]{:S(2)}, u32[]{:S(2)}) collective-permute-start(bf16[256,1536]{1,0:T(8,128)(2,1)S(1)} %get-tuple-element.86), channel_id=1, source_target_pairs={{0,3},{1,2},{2,1},{3,0},{4,7},{5,6},{6,5},{7,4},{8,11},{9,10},{10,... | collective-permute-start | bytes 2359304 | tf_op jit(solution)/shard_map/ppermute | solution.py:317
  178.5 52.0 %collective-permute-start.23 = (bf16[256,1536]{1,0:T(8,128)(2,1)S(1)}, bf16[256,1536]{1,0:T(8,128)(2,1)S(1)}, u32[]{:S(2)}, u32[]{:S(2)}) collective-permute-start(bf16[256,1536]{1,0:T(8,128)(2,1)S(1)} %get-tuple-element.80), channel_id=1, source_target_pairs={{0,1},{1,0},{2,3},{3,2},{4,5},{5,4},{6,7},{7,6},{8,9},{9,8},{10,11... | collective-permute-start | bytes 2359304 | tf_op jit(solution)/shard_map/ppermute | solution.py:317
  195.3 35.2 %copy-start.16 = (bf16[256,1536]{1,0:T(8,128)(2,1)}, bf16[256,1536]{1,0:T(8,128)(2,1)S(1)}, u32[]{:S(2)}) copy-start(bf16[256,1536]{1,0:T(8,128)(2,1)S(1)} %collective-permute-done.31.refs_3_) | copy-start | bytes 2359300
  195.3 50.7 %collective-permute-start.24 = (bf16[256,1536]{1,0:T(8,128)(2,1)S(1)}, bf16[256,1536]{1,0:T(8,128)(2,1)}, u32[]{:S(2)}, u32[]{:S(2)}) collective-permute-start(bf16[256,1536]{1,0:T(8,128)(2,1)S(1)} %get-tuple-element.81), channel_id=1, source_target_pairs={{0,2},{1,3},{2,0},{3,1},{4,6},{5,7},{6,4},{7,5},{8,10},{9,11},{10,... | collective-permute-start | bytes 2359304 | tf_op jit(solution)/shard_map/ppermute | solution.py:317
  196.8 33.7 %copy-start.17 = (bf16[256,1536]{1,0:T(8,128)(2,1)}, bf16[256,1536]{1,0:T(8,128)(2,1)S(1)}, u32[]{:S(2)}) copy-start(bf16[256,1536]{1,0:T(8,128)(2,1)S(1)} %collective-permute-done.26.refs_1_) | copy-start | bytes 2359300
  196.8 66.0 %collective-permute-start.25 = (bf16[256,1536]{1,0:T(8,128)(2,1)S(1)}, bf16[256,1536]{1,0:T(8,128)(2,1)}, u32[]{:S(2)}, u32[]{:S(2)}) collective-permute-start(bf16[256,1536]{1,0:T(8,128)(2,1)S(1)} %get-tuple-element.82), channel_id=1, source_target_pairs={{0,3},{1,2},{2,1},{3,0},{4,7},{5,6},{6,5},{7,4},{8,11},{9,10},{10,... | collective-permute-start | bytes 2359304 | tf_op jit(solution)/shard_map/ppermute | solution.py:317
  212.2 18.3 %copy-start.18 = (bf16[256,1536]{1,0:T(8,128)(2,1)}, bf16[256,1536]{1,0:T(8,128)(2,1)S(1)}, u32[]{:S(2)}) copy-start(bf16[256,1536]{1,0:T(8,128)(2,1)S(1)} %collective-permute-done.27.refs_2_) | copy-start | bytes 2359300
  212.2 54.8 %collective-permute-start.22 = (bf16[256,1536]{1,0:T(8,128)(2,1)}, bf16[256,1536]{1,0:T(8,128)(2,1)}, u32[]{:S(2)}, u32[]{:S(2)}) collective-permute-start(bf16[256,1536]{1,0:T(8,128)(2,1)} %get-tuple-element.78), channel_id=1, source_target_pairs={{0,1},{1,0},{2,3},{3,2},{4,5},{5,4},{6,7},{7,6},{8,9},{9,8},{10,11... | collective-permute-start | bytes 2359304 | tf_op jit(solution)/shard_map/ppermute | solution.py:317
  229.0 50.7 %collective-permute-start.20 = (bf16[256,1536]{1,0:T(8,128)(2,1)S(1)}, bf16[256,1536]{1,0:T(8,128)(2,1)}, u32[]{:S(2)}, u32[]{:S(2)}) collective-permute-start(bf16[256,1536]{1,0:T(8,128)(2,1)S(1)} %get-tuple-element.75), channel_id=1, source_target_pairs={{0,2},{1,3},{2,0},{3,1},{4,6},{5,7},{6,4},{7,5},{8,10},{9,11},{10,... | collective-permute-start | bytes 2359304 | tf_op jit(solution)/shard_map/ppermute | solution.py:317
  230.5 66.0 %collective-permute-start.21 = (bf16[256,1536]{1,0:T(8,128)(2,1)S(1)}, bf16[256,1536]{1,0:T(8,128)(2,1)}, u32[]{:S(2)}, u32[]{:S(2)}) collective-permute-start(bf16[256,1536]{1,0:T(8,128)(2,1)S(1)} %get-tuple-element.76), channel_id=1, source_target_pairs={{0,3},{1,2},{2,1},{3,0},{4,7},{5,6},{6,5},{7,4},{8,11},{9,10},{10,... | collective-permute-start | bytes 2359304 | tf_op jit(solution)/shard_map/ppermute | solution.py:317
  (10 other events, 20.5 us)
where the time goes:
time: 301 us; the launch traced here: 300 us
  waiting for transfers between devices  154 us (51%)
  Pallas kernels  111 us (37%)
  starting transfers between devices  25.5 us (8%)
  local copies, waits for them, and re-layouts  8.13 us (3%)
    ppermute x30, waiting for transfers between devices, swap(): return lax.ppermute(array, 'tm', [(at, at ^ peer) for at in range(groups)])  154 us
    pallas_call x4, Pallas kernels, products(): pl.pallas_call(functools.partial(product_kernel, cfg), out_shape=out_shap...  63.9 us
    pallas_call x5, Pallas kernels, pack(): pl.pallas_call(functools.partial(pack_kernel, last, sources), out_shape=[...  23.4 us
    pallas_call x5, Pallas kernels, put(): pl.pallas_call(functools.partial(place_kernel, peers, chunks, chunk), out...  19 us
    ppermute x30, starting transfers between devices, swap(): return lax.ppermute(array, 'tm', [(at, at ^ peer) for at in range(groups)])  18.8 us
    unnamed x53, local copies, waits for them, and re-layouts  7.07 us
  transfers between devices with their start and end apart: 32, of which 13 were waited for; matrix products, arithmetic and copies ran while one was open for 0% of the time, Pallas kernels for 35%

commit v1 on v0

--- a/solution.py
+++ b/solution.py
@@ -8,7 +8,7 @@
 from jax.sharding import PartitionSpec as P
 
 
-CHUNK_UNITS = 3
+CHUNK_UNITS = 6
 MiB = 1 << 20
 
 
@@ -18,16 +18,42 @@
 
 def pack_kernel(last, sources, place_ref, *refs):
     inputs, targets = refs[: -len(sources)], refs[-len(sources) :]
-    low_ref, high_ref = inputs[len(sources) :] if len(inputs) > len(sources) else (None, None)
+    low_ref, high_ref = inputs[len(sources) :]
     for peer, target in enumerate(targets):
-        value = inputs[peer][...]
-        if low_ref is not None:
-            at = sources[peer](pl.program_id(0), place_ref)
-            value = jnp.where(at < 0, low_ref[...], jnp.where(at > last, high_ref[...], value))
-        target[...] = value
-
-
-def pack(field, place, halo, peers, unit, group_units, first, count, groups):
+        at = sources[peer](pl.program_id(0), place_ref)
+        target[...] = jnp.where(
+            at < 0, low_ref[...], jnp.where(at > last, high_ref[...], inputs[peer][...])
+        )
+
+
+def copy_kernel(unit, sources, on_chip, place_ref, field_ref, *refs):
+    count = len(sources)
+    targets, sems = refs[:count], refs[-1]
+    gathered = targets if on_chip else [refs[count].at[which] for which in range(count)]
+    columns = targets[0].shape[1]
+    reads, writes = [], []
+    for which, source in enumerate(sources):
+        at = pl.multiple_of(source(0, place_ref) * unit, unit)
+        reads.append(
+            pltpu.make_async_copy(
+                field_ref.at[:, pl.ds(at, columns)], gathered[which], sems.at[0, which]
+            )
+        )
+        if not on_chip:
+            writes.append(
+                pltpu.make_async_copy(gathered[which], targets[which], sems.at[1, which])
+            )
+    for read in reads:
+        read.start()
+    for which, read in enumerate(reads):
+        read.wait()
+        if writes:
+            writes[which].start()
+    for write in writes:
+        write.wait()
+
+
+def pack(field, place, halo, peers, unit, group_units, first, count, groups, on_chip=False):
     hours_dev = field.shape[0]
     last = groups * group_units - 1
 
@@ -46,11 +72,31 @@
             (hours_dev, unit), lambda i, place: (0, jnp.clip(source(i, place), 0, last))
         )
 
+    bytes_moved = 4 * len(peers) * hours_dev * count * unit
+    if halo is None:
+        shape = (hours_dev, count * unit)
+        kind = pltpu.VMEM if on_chip else jax.ShapeDtypeStruct
+        space = pltpu.VMEM if on_chip else pl.ANY
+        scratch = [] if on_chip else [pltpu.VMEM((len(peers),) + shape, field.dtype)]
+        return pl.pallas_call(
+            functools.partial(copy_kernel, unit, sources, on_chip),
+            out_shape=[kind(shape, field.dtype) for _ in peers],
+            grid_spec=pltpu.PrefetchScalarGridSpec(
+                num_scalar_prefetch=1,
+                grid=(),
+                in_specs=[pl.BlockSpec(memory_space=pl.ANY)],
+                out_specs=[pl.BlockSpec(memory_space=space) for _ in peers],
+                scratch_shapes=scratch + [pltpu.SemaphoreType.DMA((2, len(peers)))],
+            ),
+            cost_estimate=pl.CostEstimate(
+                flops=0, transcendentals=0, bytes_accessed=bytes_moved
+            ),
+            name="pack",
+        )(place, field)
     in_specs = [spec(source) for source in sources]
     operands = [field] * len(peers)
-    if halo is not None:
-        in_specs += [pl.BlockSpec((hours_dev, unit), lambda i, place: (0, 0))] * 2
-        operands += list(halo)
+    in_specs += [pl.BlockSpec((hours_dev, unit), lambda i, place: (0, 0))] * 2
+    operands += list(halo)
     return pl.pallas_call(
         functools.partial(pack_kernel, last, sources),
         out_shape=[jax.ShapeDtypeStruct((hours_dev, count * unit), field.dtype) for _ in peers],
@@ -63,7 +109,7 @@
         cost_estimate=pl.CostEstimate(
             flops=0,
             transcendentals=0,
-            bytes_accessed=4 * len(peers) * hours_dev * count * unit,
+            bytes_accessed=bytes_moved,
         ),
         name="pack",
     )(place, *operands)
@@ -265,10 +311,12 @@
         copy.wait()
 
 
-def put(result, pieces, peers, place, cells_dev, chunks, chunk):
+def put(result, pieces, peers, place, cells_dev, chunks, chunk, on_chip):
     hours_dev, columns = pieces[0].shape
     in_specs = [pl.BlockSpec(memory_space=pltpu.VMEM)] * len(pieces)
     operands = list(pieces)
+    if on_chip:
+        operands = [pltpu.with_memory_space_constraint(piece, pltpu.VMEM) for piece in pieces]
     aliases = {}
     if result is not None:
         in_specs += [pl.BlockSpec(memory_space=pl.ANY)]
@@ -324,7 +372,7 @@
     backward = [(to, at) for at, to in forward]
     peers = list(range(groups))
 
-    first_sent = pack(field, place, None, peers, unit, group_units, 0, 1, groups)
+    first_sent = pack(field, place, None, peers, unit, group_units, 0, 1, groups, True)
     first = swap_all(first_sent)
     low = lax.ppermute(field[:, cells_dev - unit :], "space", forward)
     high = lax.ppermute(field[:, :unit], "space", backward)
@@ -348,12 +396,13 @@
         )
         returned.append(swap_all(outs))
     for chunk in range(chunks):
-        near, far = (peers, []) if chunk < chunks - 1 else (peers[:2], peers[2:])
-        for listed in (near, far):
+        closing = chunk == chunks - 1
+        parts = [peers[:2], peers[:2:-1], peers[2:3]] if closing else [peers]
+        for part, listed in enumerate(parts):
             if listed:
                 result = put(
                     result, [returned[chunk][peer] for peer in listed], listed, place,
-                    cells_dev, chunks, chunk,
+                    cells_dev, chunks, chunk, closing and part > 0,
                 )
     return result
 

time: 301 us -> 314 us (1.043)
  waiting for transfers between devices: 154 us -> 201 us
  Pallas kernels: 111 us -> 88 us
  starting transfers between devices: 25.5 us -> 16.4 us
    ppermute x30 -> x18, waiting for transfers between devices: 154 us -> 191 us  [swap(): return lax.ppermute(array, 'tm', [(at, at ^ peer) for at in range(groups)])]
    pallas_call x5 -> x1, Pallas kernels: 23.4 us -> 8 us  [pack(): pl.pallas_call(functools.partial(pack_kernel, last, sources), out_shape=[...]
    pallas_call x4 -> x2, Pallas kernels: 63.9 us -> 53.6 us  [products(): pl.pallas_call(functools.partial(product_kernel, cfg), out_shape=out_shap...]
    ppermute x1, waiting for transfers between devices: 0.01 us -> 10.2 us  [per_device(): high = lax.ppermute(field[:, :unit], 'space', backward)]
    ppermute x30 -> x18, starting transfers between devices: 18.8 us -> 10.5 us  [swap(): return lax.ppermute(array, 'tm', [(at, at ^ peer) for at in range(groups)])]
    pallas_call x0 -> x2, Pallas kernels: none -> 7.9 us  [pack(): pl.pallas_call(functools.partial(copy_kernel, unit, sources, on_chip), ou...]
    pallas_call x5 -> x4, Pallas kernels: 19 us -> 14.1 us  [put(): pl.pallas_call(functools.partial(place_kernel, peers, chunks, chunk), out...]
    unnamed x53 -> x23, local copies, waits for them, and re-layouts: 7.07 us -> 4.85 us
  transfers between devices with their start and end apart: 32 -> 20, of which waited for: 13 -> 10; matrix products, arithmetic and copies ran while one was open for 0% -> 0% of each run, Pallas kernels for 35% -> 25%
where the time goes in v1:
time: 314 us; the launch traced here: 312 us
  waiting for transfers between devices  201 us (64%)
  Pallas kernels  88 us (28%)
  starting transfers between devices  16.4 us (5%)
  local copies, waits for them, and re-layouts  5.92 us (2%)
    ppermute x18, waiting for transfers between devices, swap(): return lax.ppermute(array, 'tm', [(at, at ^ peer) for at in range(groups)])  191 us
    pallas_call x2, Pallas kernels, products(): pl.pallas_call(functools.partial(product_kernel, cfg), out_shape=out_shap...  53.6 us
    pallas_call x4, Pallas kernels, put(): pl.pallas_call(functools.partial(place_kernel, peers, chunks, chunk), out...  14.1 us
    ppermute x18, starting transfers between devices, swap(): return lax.ppermute(array, 'tm', [(at, at ^ peer) for at in range(groups)])  10.5 us
    ppermute x1, waiting for transfers between devices, per_device(): high = lax.ppermute(field[:, :unit], 'space', backward)  10.2 us
    pallas_call x1, Pallas kernels, pack(): pl.pallas_call(functools.partial(pack_kernel, last, sources), out_shape=[...  8 us
    pallas_call x2, Pallas kernels, pack(): pl.pallas_call(functools.partial(copy_kernel, unit, sources, on_chip), ou...  7.9 us
  transfers between devices with their start and end apart: 20, of which 10 were waited for; matrix products, arithmetic and copies ran while one was open for 0% of the time, Pallas kernels for 25%

profile of v1, /device:TPU:16, one launch (start us, length us, event | category | flops | bytes accessed | tf_op | source)
XLA Modules:
  0.0 312.0 jit_solution(10128504929073217653)
XLA Ops:
  0.0 0.6 pad_add_fusion.place_ref
  0.6 1.9 pack.3
  2.6 0.0 copy-start.7
  2.6 6.0 %pack.4 = (bf16[256,3072]{1,0:T(8,128)(2,1)}, bf16[256,3072]{1,0:T(8,128)(2,1)}, bf16[256,3072]{1,0:T(8,128)(2,1)}, bf16[256,3072]{1,0:T(8,128)(2,1)}) custom-call(s32[5]{0:T(128)} %pad_add_fusion.place_ref, bf16[256,24576]{1,0:T(8,128)(2,1)} %refs_3_.1), custom_call_target="tpu_custom_call" | custom-call | bytes 12582912 | tf_op jit(solution)/shard_map/pack/pallas_call | solution.py:81
  8.6 0.1 collective-permute-start.5
  8.7 1.6 collective-permute-start.6
  10.2 0.3 collective-permute-start.7
  10.5 1.1 fusion
  11.6 3.3 %collective-permute-start.1 = (bf16[256,512]{1,0:T(8,128)(2,1)S(1)}, bf16[256,512]{1,0:T(8,128)(2,1)S(1)}, u32[]{:S(2)}, u32[]{:S(2)}) collective-permute-start(bf16[256,512]{1,0:T(8,128)(2,1)S(1)} %get-tuple-element.51), channel_id=1, source_target_pairs={{4,0},{8,4},{12,8},{16,12},{20,16},{24,20},{28,24},{5,1},{9,5},{13... | collective-permute-start | bytes 786440 | tf_op jit(solution)/shard_map/ppermute | solution.py:378
  14.9 2.6 collective-permute-start
  17.4 10.2 %collective-permute-done.1.refs_5_ = bf16[256,512]{1,0:T(8,128)(2,1)S(1)} collective-permute-done((bf16[256,512]{1,0:T(8,128)(2,1)S(1)}, bf16[256,512]{1,0:T(8,128)(2,1)S(1)}, u32[]{:S(2)}, u32[]{:S(2)}) %collective-permute-start.1) | collective-permute-done | bytes 262176 | tf_op jit(solution)/shard_map/ppermute | solution.py:378
  27.7 1.5 collective-permute-start.11
  29.2 0.0 collective-permute-done.refs_4_
  29.2 0.0 collective-permute-start.9
  29.2 56.3 %collective-permute-done.11.refs_10_ = bf16[256,512]{1,0:T(8,128)(2,1)S(1)} collective-permute-done((bf16[256,512]{1,0:T(8,128)(2,1)S(1)}, bf16[256,512]{1,0:T(8,128)(2,1)S(1)}, u32[]{:S(2)}, u32[]{:S(2)}) %collective-permute-start.11) | collective-permute-done | bytes 262176 | tf_op jit(solution)/shard_map/ppermute | solution.py:365
  85.5 4.5 %collective-permute-done.9.refs_11_ = bf16[256,512]{1,0:T(8,128)(2,1)S(1)} collective-permute-done((bf16[256,512]{1,0:T(8,128)(2,1)S(1)}, bf16[256,512]{1,0:T(8,128)(2,1)S(1)}, u32[]{:S(2)}, u32[]{:S(2)}) %collective-permute-start.9) | collective-permute-done | bytes 262176 | tf_op jit(solution)/shard_map/ppermute | solution.py:365
  90.1 0.4 collective-permute-start.8
  90.4 0.1 collective-permute-start.12
  90.6 1.0 collective-permute-done.8.refs_5_
  91.6 0.4 collective-permute-start.10
  92.0 0.1 copy.10.neighbours_ref
  92.1 4.5 %order.1.cov_ref = bf16[1024,1024]{1,0:T(8,128)(2,1)} custom-call(s32[5]{0:T(128)} %pad_add_fusion.place_ref, bf16[1024,1024]{1,0:T(8,128)(2,1)} %source.1), custom_call_target="tpu_custom_call" | custom-call | tf_op jit(solution)/shard_map/order/pallas_call | solution.py:125
  96.5 0.0 copy-start.3
  96.5 8.0 %pack.5 = (bf16[256,3072]{1,0:T(8,128)(2,1)}, bf16[256,3072]{1,0:T(8,128)(2,1)}, bf16[256,3072]{1,0:T(8,128)(2,1)}, bf16[256,3072]{1,0:T(8,128)(2,1)}) custom-call(s32[5]{0:T(128)} %pad_add_fusion.place_ref, bf16[256,24576]{1,0:T(8,128)(2,1)} %refs_3_.1, bf16[256,24576]{1,0:T(8,128)(2,1)} %refs_3_.1, bf16[256,24576]{1,0:T(8,128)(2,1)} %refs_3_.1, ...), custom_call_target="tpu_custom_call" | custom-call | bytes 12582912 | tf_op jit(solution)/shard_map/pack/pallas_call | solution.py:100
  104.5 0.1 collective-permute-start.2
  104.7 1.6 collective-permute-start.3
  106.3 0.2 collective-permute-start.4
  106.5 28.3 %products.2 = (bf16[256,3072]{1,0:T(8,128)(2,1)S(1)}, bf16[256,3072]{1,0:T(8,128)(2,1)S(1)}, bf16[256,3072]{1,0:T(8,128)(2,1)}, bf16[256,3072]{1,0:T(8,128)(2,1)}, bf16[1024,1024]{1,0:T(8,128)(2,1)}) custom-call(s32[5]{0:T(128)S(1)} %copy-done.2, s32[48,9]{1,0:T(8,128)S(1)} %copy.10.neighbours_ref, s32[48]{0:T(128)S(1)} %copy-done.3, ...), custom_call_target="tpu_custom_call" | custom-call | flops 16642998272 | bytes 21757952 | tf_op jit(solution)/shard_map/products/pallas_call | solution.py:267
  134.8 1.2 copy-done
  136.0 0.4 collective-permute-start.17
  136.4 1.6 collective-permute-start.18
  138.0 4.1 %collective-permute-done.3.refs_2_ = bf16[256,3072]{1,0:T(8,128)(2,1)S(1)} collective-permute-done((bf16[256,3072]{1,0:T(8,128)(2,1)}, bf16[256,3072]{1,0:T(8,128)(2,1)S(1)}, u32[]{:S(2)}, u32[]{:S(2)}) %collective-permute-start.3) | collective-permute-done | bytes 1572896 | tf_op jit(solution)/shard_map/ppermute | solution.py:365
  142.2 32.9 %collective-permute-done.4.refs_3_ = bf16[256,3072]{1,0:T(8,128)(2,1)S(1)} collective-permute-done((bf16[256,3072]{1,0:T(8,128)(2,1)}, bf16[256,3072]{1,0:T(8,128)(2,1)S(1)}, u32[]{:S(2)}, u32[]{:S(2)}) %collective-permute-start.4) | collective-permute-done | bytes 1572896 | tf_op jit(solution)/shard_map/ppermute | solution.py:365
  175.1 1.1 copy-done.10
  176.2 25.3 %products.3 = (bf16[256,3072]{1,0:T(8,128)(2,1)S(1)}, bf16[256,3072]{1,0:T(8,128)(2,1)}, bf16[256,3072]{1,0:T(8,128)(2,1)}, bf16[256,3072]{1,0:T(8,128)(2,1)}) custom-call(s32[5]{0:T(128)S(1)} %copy-done.2, s32[48,9]{1,0:T(8,128)S(1)} %copy.10.neighbours_ref, s32[48]{0:T(128)S(1)} %copy-done.3, bf16[1024,1024]{1,0:T(8,128)(2,1)} %order.1.cov_ref, ...), custom_call_target="tpu_custom_call" | custom-call | flops 14495514624 | bytes 19660800 | tf_op jit(solution)/shard_map/products/pallas_call | solution.py:267
  201.5 1.2 copy-done.1
  202.7 0.7 collective-permute-start.16
  203.4 1.2 collective-permute-start.15
  204.6 1.2 copy-done.4
  205.7 0.4 collective-permute-start.14
  206.2 3.5 %collective-permute-done.18.refs_2_ = bf16[256,3072]{1,0:T(8,128)(2,1)} collective-permute-done((bf16[256,3072]{1,0:T(8,128)(2,1)}, bf16[256,3072]{1,0:T(8,128)(2,1)}, u32[]{:S(2)}, u32[]{:S(2)}) %collective-permute-start.18) | collective-permute-done | bytes 1572896 | tf_op jit(solution)/shard_map/ppermute | solution.py:365
  209.7 32.8 %collective-permute-done.19.refs_3_ = bf16[256,3072]{1,0:T(8,128)(2,1)} collective-permute-done((bf16[256,3072]{1,0:T(8,128)(2,1)}, bf16[256,3072]{1,0:T(8,128)(2,1)}, u32[]{:S(2)}, u32[]{:S(2)}) %collective-permute-start.19) | collective-permute-done | bytes 1572896 | tf_op jit(solution)/shard_map/ppermute | solution.py:365
  242.5 6.2 %place.4.refs_2_ = bf16[256,24576]{1,0:T(8,128)(2,1)} custom-call(s32[5]{0:T(128)} %pad_add_fusion.place_ref, bf16[256,3072]{1,0:T(8,128)(2,1)} %copy-done, bf16[256,3072]{1,0:T(8,128)(2,1)} %copy-done.4, bf16[256,3072]{1,0:T(8,128)(2,1)} %collective-permute-done.18.refs_2_, bf16[256,3072]{1,0:T(8,128)(2,1)} %collective-permute-done.19.refs_3_), custom_call_target="tpu_custom_call" | custom-call | bytes 12582912 | tf_op jit(solution)/shard_map/place/pallas_call | solution.py:325
  248.7 4.2 %place.5.refs_1_ = bf16[256,24576]{1,0:T(8,128)(2,1)} custom-call(s32[5]{0:T(128)} %pad_add_fusion.place_ref, bf16[256,3072]{1,0:T(8,128)(2,1)} %copy-done.1, bf16[256,3072]{1,0:T(8,128)(2,1)} %collective-permute-done.16.refs_1_, bf16[256,24576]{1,0:T(8,128)(2,1)} %place.4.refs_2_), custom_call_target="tpu_custom_call", output_to_operand_aliasing={{}: (3, {})} | custom-call | bytes 6291456 | tf_op jit(solution)/shard_map/place/pallas_call | solution.py:325
  253.0 23.2 %collective-permute-done.15.refs_0_ = bf16[256,3072]{1,0:T(8,128)(2,1)S(1)} collective-permute-done((bf16[256,3072]{1,0:T(8,128)(2,1)}, bf16[256,3072]{1,0:T(8,128)(2,1)S(1)}, u32[]{:S(2)}, u32[]{:S(2)}) %collective-permute-start.15) | collective-permute-done | bytes 1572896 | tf_op jit(solution)/shard_map/ppermute | solution.py:365
  276.2 1.8 place.6.refs_1_
  278.0 32.1 %collective-permute-done.14.refs_0_ = bf16[256,3072]{1,0:T(8,128)(2,1)S(1)} collective-permute-done((bf16[256,3072]{1,0:T(8,128)(2,1)}, bf16[256,3072]{1,0:T(8,128)(2,1)S(1)}, u32[]{:S(2)}, u32[]{:S(2)}) %collective-permute-start.14) | collective-permute-done | bytes 1572896 | tf_op jit(solution)/shard_map/ppermute | solution.py:365
  310.2 1.8 place.7
  (28 shorter events, 0.1 us)
Async XLA Ops:
  2.6 89.4 %copy-start.7 = (s32[48,9]{0,1:T(8,128)S(1)}, s32[48,9]{0,1:T(8,128)}, u32[]{:S(2)}) copy-start(s32[48,9]{0,1:T(8,128)} %param.8) | copy-start | bytes 5188
  8.6 97.7 %collective-permute-start.5 = (bf16[256,3072]{1,0:T(8,128)(2,1)}, bf16[256,3072]{1,0:T(8,128)(2,1)}, u32[]{:S(2)}, u32[]{:S(2)}) collective-permute-start(bf16[256,3072]{1,0:T(8,128)(2,1)} %get-tuple-element.37), channel_id=1, source_target_pairs={{0,1},{1,0},{2,3},{3,2},{4,5},{5,4},{6,7},{7,6},{8,9},{9,8},{10,11... | collective-permute-start | bytes 4718600 | tf_op jit(solution)/shard_map/ppermute | solution.py:365
  8.7 97.8 %collective-permute-start.6 = (bf16[256,3072]{1,0:T(8,128)(2,1)}, bf16[256,3072]{1,0:T(8,128)(2,1)}, u32[]{:S(2)}, u32[]{:S(2)}) collective-permute-start(bf16[256,3072]{1,0:T(8,128)(2,1)} %get-tuple-element.38), channel_id=1, source_target_pairs={{0,2},{1,3},{2,0},{3,1},{4,6},{5,7},{6,4},{7,5},{8,10},{9,11},{10,... | collective-permute-start | bytes 4718600 | tf_op jit(solution)/shard_map/ppermute | solution.py:365
  10.2 96.2 %collective-permute-start.7 = (bf16[256,3072]{1,0:T(8,128)(2,1)}, bf16[256,3072]{1,0:T(8,128)(2,1)}, u32[]{:S(2)}, u32[]{:S(2)}) collective-permute-start(bf16[256,3072]{1,0:T(8,128)(2,1)} %get-tuple-element.30), channel_id=1, source_target_pairs={{0,3},{1,2},{2,1},{3,0},{4,7},{5,6},{6,5},{7,4},{8,11},{9,10},{10,... | collective-permute-start | bytes 4718600 | tf_op jit(solution)/shard_map/ppermute | solution.py:365
  11.6 16.1 %collective-permute-start.1 = (bf16[256,512]{1,0:T(8,128)(2,1)S(1)}, bf16[256,512]{1,0:T(8,128)(2,1)S(1)}, u32[]{:S(2)}, u32[]{:S(2)}) collective-permute-start(bf16[256,512]{1,0:T(8,128)(2,1)S(1)} %get-tuple-element.51), channel_id=1, source_target_pairs={{4,0},{8,4},{12,8},{16,12},{20,16},{24,20},{28,24},{5,1},{9,5},{13... | collective-permute-start | bytes 786440 | tf_op jit(solution)/shard_map/ppermute | solution.py:378
  14.9 14.3 %collective-permute-start = (bf16[256,512]{1,0:T(8,128)(2,1)S(1)}, bf16[256,512]{1,0:T(8,128)(2,1)S(1)}, u32[]{:S(2)}, u32[]{:S(2)}) collective-permute-start(bf16[256,512]{1,0:T(8,128)(2,1)S(1)} %get-tuple-element.52), channel_id=1, source_target_pairs={{0,4},{4,8},{8,12},{12,16},{16,20},{20,24},{24,28},{1,5},{5,9},{9,... | collective-permute-start | bytes 786440 | tf_op jit(solution)/shard_map/ppermute | solution.py:377
  27.7 68.9 %copy-start.5 = (bf16[256,512]{1,0:T(8,128)(2,1)}, bf16[256,512]{1,0:T(8,128)(2,1)S(1)}, u32[]{:S(2)}) copy-start(bf16[256,512]{1,0:T(8,128)(2,1)S(1)} %collective-permute-done.1.refs_5_) | copy-start | bytes 786436
  27.7 57.9 %collective-permute-start.11 = (bf16[256,512]{1,0:T(8,128)(2,1)S(1)}, bf16[256,512]{1,0:T(8,128)(2,1)S(1)}, u32[]{:S(2)}, u32[]{:S(2)}) collective-permute-start(bf16[256,512]{1,0:T(8,128)(2,1)S(1)} %get-tuple-element.41), channel_id=1, source_target_pairs={{0,2},{1,3},{2,0},{3,1},{4,6},{5,7},{6,4},{7,5},{8,10},{9,11},{10,... | collective-permute-start | bytes 786440 | tf_op jit(solution)/shard_map/ppermute | solution.py:365
  29.2 67.3 %copy-start.6 = (bf16[256,512]{1,0:T(8,128)(2,1)}, bf16[256,512]{1,0:T(8,128)(2,1)S(1)}, u32[]{:S(2)}) copy-start(bf16[256,512]{1,0:T(8,128)(2,1)S(1)} %collective-permute-done.refs_4_) | copy-start | bytes 786436
  29.2 60.9 %collective-permute-start.9 = (bf16[256,512]{1,0:T(8,128)(2,1)S(1)}, bf16[256,512]{1,0:T(8,128)(2,1)S(1)}, u32[]{:S(2)}, u32[]{:S(2)}) collective-permute-start(bf16[256,512]{1,0:T(8,128)(2,1)S(1)} %get-tuple-element.28), channel_id=1, source_target_pairs={{0,3},{1,2},{2,1},{3,0},{4,7},{5,6},{6,5},{7,4},{8,11},{9,10},{10,... | collective-permute-start | bytes 786440 | tf_op jit(solution)/shard_map/ppermute | solution.py:365
  85.5 4.9 %collective-permute-start.13 = (bf16[256,512]{1,0:T(8,128)(2,1)S(1)}, bf16[256,512]{1,0:T(8,128)(2,1)S(1)}, u32[]{:S(2)}, u32[]{:S(2)}) collective-permute-start(bf16[256,512]{1,0:T(8,128)(2,1)S(1)} %get-tuple-element.39.refs_4_), channel_id=1, source_target_pairs={{0,1},{1,0},{2,3},{3,2},{4,5},{5,4},{6,7},{7,6},{8,9},{9,8},{10,11... | collective-permute-start | bytes 786440 | tf_op jit(solution)/shard_map/ppermute | solution.py:365
  90.1 1.5 collective-permute-start.8
  90.4 14.1 %collective-permute-start.12 = (bf16[256,512]{1,0:T(8,128)(2,1)S(1)}, bf16[256,512]{1,0:T(8,128)(2,1)S(1)}, u32[]{:S(2)}, u32[]{:S(2)}) collective-permute-start(bf16[256,512]{1,0:T(8,128)(2,1)S(1)} %collective-permute-done.11.refs_10_), channel_id=1, source_target_pairs={{0,1},{1,0},{2,3},{3,2},{4,5},{5,4},{6,7},{7,6},{8,9},{9,8},{10,11... | collective-permute-start | bytes 786440 | tf_op jit(solution)/shard_map/ppermute | solution.py:365
  91.6 13.1 %collective-permute-start.10 = (bf16[256,512]{1,0:T(8,128)(2,1)S(1)}, bf16[256,512]{1,0:T(8,128)(2,1)S(1)}, u32[]{:S(2)}, u32[]{:S(2)}) collective-permute-start(bf16[256,512]{1,0:T(8,128)(2,1)S(1)} %collective-permute-done.9.refs_11_), channel_id=1, source_target_pairs={{0,1},{1,0},{2,3},{3,2},{4,5},{5,4},{6,7},{7,6},{8,9},{9,8},{10,11... | collective-permute-start | bytes 786440 | tf_op jit(solution)/shard_map/ppermute | solution.py:365
  96.5 10.0 %copy-start.2 = (s32[5]{0:T(128)S(1)}, s32[5]{0:T(128)}, u32[]{:S(2)}) copy-start(s32[5]{0:T(128)} %pad_add_fusion.place_ref) | copy-start | bytes 64
  96.5 10.0 %copy-start.3 = (s32[48]{0:T(128)S(1)}, s32[48]{0:T(128)}, u32[]{:S(2)}) copy-start(s32[48]{0:T(128)} %counts_ref.3) | copy-start | bytes 580
  104.5 33.5 %collective-permute-start.2 = (bf16[256,3072]{1,0:T(8,128)(2,1)}, bf16[256,3072]{1,0:T(8,128)(2,1)S(1)}, u32[]{:S(2)}, u32[]{:S(2)}) collective-permute-start(bf16[256,3072]{1,0:T(8,128)(2,1)} %get-tuple-element.33), channel_id=1, source_target_pairs={{0,1},{1,0},{2,3},{3,2},{4,5},{5,4},{6,7},{7,6},{8,9},{9,8},{10,11... | collective-permute-start | bytes 4718600 | tf_op jit(solution)/shard_map/ppermute | solution.py:365
  104.7 37.5 %collective-permute-start.3 = (bf16[256,3072]{1,0:T(8,128)(2,1)}, bf16[256,3072]{1,0:T(8,128)(2,1)S(1)}, u32[]{:S(2)}, u32[]{:S(2)}) collective-permute-start(bf16[256,3072]{1,0:T(8,128)(2,1)} %get-tuple-element.34), channel_id=1, source_target_pairs={{0,2},{1,3},{2,0},{3,1},{4,6},{5,7},{6,4},{7,5},{8,10},{9,11},{10,... | collective-permute-start | bytes 4718600 | tf_op jit(solution)/shard_map/ppermute | solution.py:365
  106.3 68.8 %collective-permute-start.4 = (bf16[256,3072]{1,0:T(8,128)(2,1)}, bf16[256,3072]{1,0:T(8,128)(2,1)S(1)}, u32[]{:S(2)}, u32[]{:S(2)}) collective-permute-start(bf16[256,3072]{1,0:T(8,128)(2,1)} %get-tuple-element.35), channel_id=1, source_target_pairs={{0,3},{1,2},{2,1},{3,0},{4,7},{5,6},{6,5},{7,4},{8,11},{9,10},{10,... | collective-permute-start | bytes 4718600 | tf_op jit(solution)/shard_map/ppermute | solution.py:365
  134.8 1.2 copy-start
  136.0 68.5 %collective-permute-start.17 = (bf16[256,3072]{1,0:T(8,128)(2,1)S(1)}, bf16[256,3072]{1,0:T(8,128)(2,1)S(1)}, u32[]{:S(2)}, u32[]{:S(2)}) collective-permute-start(bf16[256,3072]{1,0:T(8,128)(2,1)S(1)} %get-tuple-element.48), channel_id=1, source_target_pairs={{0,1},{1,0},{2,3},{3,2},{4,5},{5,4},{6,7},{7,6},{8,9},{9,8},{10,11... | collective-permute-start | bytes 4718600 | tf_op jit(solution)/shard_map/ppermute | solution.py:365
  136.4 73.2 %collective-permute-start.18 = (bf16[256,3072]{1,0:T(8,128)(2,1)}, bf16[256,3072]{1,0:T(8,128)(2,1)}, u32[]{:S(2)}, u32[]{:S(2)}) collective-permute-start(bf16[256,3072]{1,0:T(8,128)(2,1)} %get-tuple-element.49), channel_id=1, source_target_pairs={{0,2},{1,3},{2,0},{3,1},{4,6},{5,7},{6,4},{7,5},{8,10},{9,11},{10,... | collective-permute-start | bytes 4718600 | tf_op jit(solution)/shard_map/ppermute | solution.py:365
  138.0 37.1 %copy-start.8 = (bf16[256,3072]{1,0:T(8,128)(2,1)}, bf16[256,3072]{1,0:T(8,128)(2,1)S(1)}, u32[]{:S(2)}) copy-start(bf16[256,3072]{1,0:T(8,128)(2,1)S(1)} %collective-permute-done.2.refs_1_) | copy-start | bytes 4718596
  138.0 104.5 %collective-permute-start.19 = (bf16[256,3072]{1,0:T(8,128)(2,1)}, bf16[256,3072]{1,0:T(8,128)(2,1)}, u32[]{:S(2)}, u32[]{:S(2)}) collective-permute-start(bf16[256,3072]{1,0:T(8,128)(2,1)} %get-tuple-element.50), channel_id=1, source_target_pairs={{0,3},{1,2},{2,1},{3,0},{4,7},{5,6},{6,5},{7,4},{8,11},{9,10},{10,... | collective-permute-start | bytes 4718600 | tf_op jit(solution)/shard_map/ppermute | solution.py:365
  142.2 32.9 %copy-start.9 = (bf16[256,3072]{1,0:T(8,128)(2,1)}, bf16[256,3072]{1,0:T(8,128)(2,1)S(1)}, u32[]{:S(2)}) copy-start(bf16[256,3072]{1,0:T(8,128)(2,1)S(1)} %collective-permute-done.3.refs_2_) | copy-start | bytes 4718596
  175.1 1.1 copy-start.10
  201.5 1.2 copy-start.1
  202.7 46.0 %collective-permute-start.16 = (bf16[256,3072]{1,0:T(8,128)(2,1)}, bf16[256,3072]{1,0:T(8,128)(2,1)}, u32[]{:S(2)}, u32[]{:S(2)}) collective-permute-start(bf16[256,3072]{1,0:T(8,128)(2,1)} %get-tuple-element.46), channel_id=1, source_target_pairs={{0,1},{1,0},{2,3},{3,2},{4,5},{5,4},{6,7},{7,6},{8,9},{9,8},{10,11... | collective-permute-start | bytes 4718600 | tf_op jit(solution)/shard_map/ppermute | solution.py:365
  203.4 72.8 %collective-permute-start.15 = (bf16[256,3072]{1,0:T(8,128)(2,1)}, bf16[256,3072]{1,0:T(8,128)(2,1)S(1)}, u32[]{:S(2)}, u32[]{:S(2)}) collective-permute-start(bf16[256,3072]{1,0:T(8,128)(2,1)} %get-tuple-element.44), channel_id=1, source_target_pairs={{0,3},{1,2},{2,1},{3,0},{4,7},{5,6},{6,5},{7,4},{8,11},{9,10},{10,... | collective-permute-start | bytes 4718600 | tf_op jit(solution)/shard_map/ppermute | solution.py:365
  204.6 1.2 copy-start.4
  205.7 104.4 %collective-permute-start.14 = (bf16[256,3072]{1,0:T(8,128)(2,1)}, bf16[256,3072]{1,0:T(8,128)(2,1)S(1)}, u32[]{:S(2)}, u32[]{:S(2)}) collective-permute-start(bf16[256,3072]{1,0:T(8,128)(2,1)} %get-tuple-element.43), channel_id=1, source_target_pairs={{0,2},{1,3},{2,0},{3,1},{4,6},{5,7},{6,4},{7,5},{8,10},{9,11},{10,... | collective-permute-start | bytes 4718600 | tf_op jit(solution)/shard_map/ppermute | solution.py:365

commit v2 on v1

--- a/solution.py
+++ b/solution.py
@@ -9,6 +9,7 @@
 
 
 CHUNK_UNITS = 6
+ROW_COPIES = 4
 MiB = 1 << 20
 
 
@@ -26,7 +27,13 @@
         )
 
 
-def copy_kernel(unit, sources, on_chip, place_ref, field_ref, *refs):
+def copy_kernel(unit, sources, peers, on_chip, *refs):
+    if on_chip:
+        mine = lax.axis_index("tm")
+        place_ref = {peer: jnp.bitwise_xor(mine, peer) for peer in peers}
+        field_ref, *refs = refs
+    else:
+        place_ref, field_ref, *refs = refs
     count = len(sources)
     targets, sems = refs[:count], refs[-1]
     gathered = targets if on_chip else [refs[count].at[which] for which in range(count)]
@@ -78,11 +85,12 @@
         kind = pltpu.VMEM if on_chip else jax.ShapeDtypeStruct
         space = pltpu.VMEM if on_chip else pl.ANY
         scratch = [] if on_chip else [pltpu.VMEM((len(peers),) + shape, field.dtype)]
+        operands = [field] if on_chip else [place, field]
         return pl.pallas_call(
-            functools.partial(copy_kernel, unit, sources, on_chip),
+            functools.partial(copy_kernel, unit, sources, peers, on_chip),
             out_shape=[kind(shape, field.dtype) for _ in peers],
             grid_spec=pltpu.PrefetchScalarGridSpec(
-                num_scalar_prefetch=1,
+                num_scalar_prefetch=len(operands) - 1,
                 grid=(),
                 in_specs=[pl.BlockSpec(memory_space=pl.ANY)],
                 out_specs=[pl.BlockSpec(memory_space=space) for _ in peers],
@@ -92,7 +100,7 @@
                 flops=0, transcendentals=0, bytes_accessed=bytes_moved
             ),
             name="pack",
-        )(place, field)
+        )(*operands)
     in_specs = [spec(source) for source in sources]
     operands = [field] * len(peers)
     in_specs += [pl.BlockSpec((hours_dev, unit), lambda i, place: (0, 0))] * 2
@@ -298,13 +306,18 @@
         columns = source.shape[1]
         group = place_ref[peer]
         at = group * chunks + jnp.where(ascends(group), chunk, chunks - 1 - chunk)
-        copies.append(
-            pltpu.make_async_copy(
-                source,
-                target.at[:, pl.ds(pl.multiple_of(at * columns, columns), columns)],
-                sems.at[which],
+        rows = source.shape[0] // ROW_COPIES
+        for part in range(ROW_COPIES):
+            copies.append(
+                pltpu.make_async_copy(
+                    source.at[part * rows : (part + 1) * rows],
+                    target.at[
+                        part * rows : (part + 1) * rows,
+                        pl.ds(pl.multiple_of(at * columns, columns), columns),
+                    ],
+                    sems.at[which, part],
+                )
             )
-        )
     for copy in copies:
         copy.start()
     for copy in copies:
@@ -330,7 +343,7 @@
             grid=(),
             in_specs=in_specs,
             out_specs=pl.BlockSpec(memory_space=pl.ANY),
-            scratch_shapes=[pltpu.SemaphoreType.DMA((len(pieces),))],
+            scratch_shapes=[pltpu.SemaphoreType.DMA((len(pieces), ROW_COPIES))],
         ),
         input_output_aliases=aliases,
         cost_estimate=pl.CostEstimate(
@@ -361,18 +374,21 @@
         ]
     )
 
+    peers = list(range(groups))
+
     def swap(array, peer):
         return lax.ppermute(array, "tm", [(at, at ^ peer) for at in range(groups)])
 
     def swap_all(arrays):
-        moved = {peer: swap(arrays[peer], peer) for peer in range(groups - 1, 0, -1)}
+        moved = {peer: swap(arrays[peer], peer) for peer in peers[2:] + peers[1:2]}
         return [arrays[0]] + [moved[peer] for peer in range(1, groups)]
 
     forward = [(at, at + 1) for at in range(spaces - 1)]
     backward = [(to, at) for at, to in forward]
-    peers = list(range(groups))
-
-    first_sent = pack(field, place, None, peers, unit, group_units, 0, 1, groups, True)
+
+    far = pack(field, None, None, peers[2:], unit, group_units, 0, 1, groups, True)
+    near = pack(field, None, None, peers[:2], unit, group_units, 0, 1, groups, True)
+    first_sent = near + far
     first = swap_all(first_sent)
     low = lax.ppermute(field[:, cells_dev - unit :], "space", forward)
     high = lax.ppermute(field[:, :unit], "space", backward)
@@ -397,7 +413,7 @@
         returned.append(swap_all(outs))
     for chunk in range(chunks):
         closing = chunk == chunks - 1
-        parts = [peers[:2], peers[:2:-1], peers[2:3]] if closing else [peers]
+        parts = [peers[:2], peers[2:-1], peers[-1:]] if closing else [peers]
         for part, listed in enumerate(parts):
             if listed:
                 result = put(

time: 314 us -> 312 us (level)
    pallas_call x2 -> x3, Pallas kernels: 7.9 us -> 8.07 us  [pack(): pl.pallas_call(functools.partial(copy_kernel, unit, sources, peers, on_ch...]
  transfers between devices with their start and end apart: 20 -> 20, of which waited for: 10 -> 10; matrix products, arithmetic and copies ran while one was open for 0% -> 0% of each run, Pallas kernels for 25% -> 26%
where the time goes in v2:
time: 312 us; the launch traced here: 311 us
  waiting for transfers between devices  199 us (64%)
  Pallas kernels  88.5 us (28%)
  starting transfers between devices  16.3 us (5%)
  local copies, waits for them, and re-layouts  5.91 us (2%)
    ppermute x18, waiting for transfers between devices, swap(): return lax.ppermute(array, 'tm', [(at, at ^ peer) for at in range(groups)])  189 us
    pallas_call x2, Pallas kernels, products(): pl.pallas_call(functools.partial(product_kernel, cfg), out_shape=out_shap...  53.6 us
    pallas_call x4, Pallas kernels, put(): pl.pallas_call(functools.partial(place_kernel, peers, chunks, chunk), out...  14.2 us
    ppermute x18, starting transfers between devices, swap(): return lax.ppermute(array, 'tm', [(at, at ^ peer) for at in range(groups)])  10.4 us
    ppermute x1, waiting for transfers between devices, per_device(): high = lax.ppermute(field[:, :unit], 'space', backward)  10.2 us
    pallas_call x1, Pallas kernels, pack(): pl.pallas_call(functools.partial(pack_kernel, last, sources), out_shape=[...  8.1 us
    pallas_call x3, Pallas kernels, pack(): pl.pallas_call(functools.partial(copy_kernel, unit, sources, peers, on_ch...  8.07 us
  transfers between devices with their start and end apart: 20, of which 10 were waited for; matrix products, arithmetic and copies ran while one was open for 0% of the time, Pallas kernels for 26%

profile of v2, /device:TPU:16, one launch (start us, length us, event | category | flops | bytes accessed | tf_op | source)
XLA Modules:
  0.0 310.5 jit_solution(4278986946486006017)
XLA Ops:
  0.0 1.1 pack.4
  1.1 0.6 pad_add_fusion.place_ref.refs_0_
  1.7 5.8 %pack.5 = (bf16[256,3072]{1,0:T(8,128)(2,1)}, bf16[256,3072]{1,0:T(8,128)(2,1)}, bf16[256,3072]{1,0:T(8,128)(2,1)}, bf16[256,3072]{1,0:T(8,128)(2,1)}) custom-call(s32[5]{0:T(128)} %pad_add_fusion.place_ref.refs_0_, bf16[256,24576]{1,0:T(8,128)(2,1)} %refs_0_.5), custom_call_target="tpu_custom_call" | custom-call | bytes 12582912 | tf_op jit(solution)/shard_map/pack/pallas_call | solution.py:89
  7.6 0.1 collective-permute-start.5
  7.7 1.6 collective-permute-start.6
  9.2 0.3 collective-permute-start.7
  9.5 1.1 fusion
  10.6 3.3 %collective-permute-start.1 = (bf16[256,512]{1,0:T(8,128)(2,1)S(1)}, bf16[256,512]{1,0:T(8,128)(2,1)S(1)}, u32[]{:S(2)}, u32[]{:S(2)}) collective-permute-start(bf16[256,512]{1,0:T(8,128)(2,1)S(1)} %get-tuple-element.51), channel_id=1, source_target_pairs={{4,0},{8,4},{12,8},{16,12},{20,16},{24,20},{28,24},{5,1},{9,5},{13... | collective-permute-start | bytes 786440 | tf_op jit(solution)/shard_map/ppermute | solution.py:394
  13.9 2.6 collective-permute-start
  16.4 10.2 %collective-permute-done.1.refs_5_ = bf16[256,512]{1,0:T(8,128)(2,1)S(1)} collective-permute-done((bf16[256,512]{1,0:T(8,128)(2,1)S(1)}, bf16[256,512]{1,0:T(8,128)(2,1)S(1)}, u32[]{:S(2)}, u32[]{:S(2)}) %collective-permute-start.1) | collective-permute-done | bytes 262176 | tf_op jit(solution)/shard_map/ppermute | solution.py:394
  26.7 1.5 collective-permute-start.11
  28.2 0.0 collective-permute-done.refs_4_
  28.2 0.0 collective-permute-start.9
  28.2 1.2 pack.7
  29.4 55.1 %collective-permute-done.11.refs_10_ = bf16[256,512]{1,0:T(8,128)(2,1)S(1)} collective-permute-done((bf16[256,512]{1,0:T(8,128)(2,1)S(1)}, bf16[256,512]{1,0:T(8,128)(2,1)S(1)}, u32[]{:S(2)}, u32[]{:S(2)}) %collective-permute-start.11) | collective-permute-done | bytes 262176 | tf_op jit(solution)/shard_map/ppermute | solution.py:380
  84.5 4.5 %collective-permute-done.9.refs_11_ = bf16[256,512]{1,0:T(8,128)(2,1)S(1)} collective-permute-done((bf16[256,512]{1,0:T(8,128)(2,1)S(1)}, bf16[256,512]{1,0:T(8,128)(2,1)S(1)}, u32[]{:S(2)}, u32[]{:S(2)}) %collective-permute-start.9) | collective-permute-done | bytes 262176 | tf_op jit(solution)/shard_map/ppermute | solution.py:380
  89.1 0.4 collective-permute-start.8
  89.4 0.0 collective-permute-done.13.refs_9_
  89.4 0.1 collective-permute-start.12
  89.6 1.0 collective-permute-done.8.refs_5_
  90.6 0.4 collective-permute-start.10
  91.0 0.1 copy.10.neighbours_ref
  91.0 4.5 %order.1.cov_ref = bf16[1024,1024]{1,0:T(8,128)(2,1)} custom-call(s32[5]{0:T(128)} %pad_add_fusion.place_ref.refs_0_, bf16[1024,1024]{1,0:T(8,128)(2,1)} %source.1), custom_call_target="tpu_custom_call" | custom-call | tf_op jit(solution)/shard_map/order/pallas_call | solution.py:133
  95.5 8.1 %pack.6 = (bf16[256,3072]{1,0:T(8,128)(2,1)}, bf16[256,3072]{1,0:T(8,128)(2,1)}, bf16[256,3072]{1,0:T(8,128)(2,1)}, bf16[256,3072]{1,0:T(8,128)(2,1)}) custom-call(s32[5]{0:T(128)} %pad_add_fusion.place_ref.refs_0_, bf16[256,24576]{1,0:T(8,128)(2,1)} %refs_0_.5, bf16[256,24576]{1,0:T(8,128)(2,1)} %refs_0_.5, bf16[256,24576]{1,0:T(8,128)(2,1)} %refs_0_.5, ...), custom_call_target="tpu_custom_call" | custom-call | bytes 12582912 | tf_op jit(solution)/shard_map/pack/pallas_call | solution.py:108
  103.6 0.1 collective-permute-start.2
  103.7 0.0 collective-permute-done.10.refs_6_
  103.7 1.6 collective-permute-start.3
  105.3 0.2 collective-permute-start.4
  105.6 28.3 %products.2 = (bf16[256,3072]{1,0:T(8,128)(2,1)S(1)}, bf16[256,3072]{1,0:T(8,128)(2,1)S(1)}, bf16[256,3072]{1,0:T(8,128)(2,1)}, bf16[256,3072]{1,0:T(8,128)(2,1)}, bf16[1024,1024]{1,0:T(8,128)(2,1)}) custom-call(s32[5]{0:T(128)S(1)} %copy-done.2, s32[48,9]{1,0:T(8,128)S(1)} %copy.10.neighbours_ref, s32[48]{0:T(128)S(1)} %copy-done.3, ...), custom_call_target="tpu_custom_call" | custom-call | flops 16642998272 | bytes 21757952 | tf_op jit(solution)/shard_map/products/pallas_call | solution.py:275
  133.9 1.2 copy-done
  135.1 0.4 collective-permute-start.17
  135.5 1.6 collective-permute-start.18
  137.1 4.2 %collective-permute-done.3.refs_2_ = bf16[256,3072]{1,0:T(8,128)(2,1)S(1)} collective-permute-done((bf16[256,3072]{1,0:T(8,128)(2,1)}, bf16[256,3072]{1,0:T(8,128)(2,1)S(1)}, u32[]{:S(2)}, u32[]{:S(2)}) %collective-permute-start.3) | collective-permute-done | bytes 1572896 | tf_op jit(solution)/shard_map/ppermute | solution.py:380
  141.2 32.9 %collective-permute-done.4.refs_3_ = bf16[256,3072]{1,0:T(8,128)(2,1)S(1)} collective-permute-done((bf16[256,3072]{1,0:T(8,128)(2,1)}, bf16[256,3072]{1,0:T(8,128)(2,1)S(1)}, u32[]{:S(2)}, u32[]{:S(2)}) %collective-permute-start.4) | collective-permute-done | bytes 1572896 | tf_op jit(solution)/shard_map/ppermute | solution.py:380
  174.2 1.2 copy-done.10
  175.3 25.3 %products.3 = (bf16[256,3072]{1,0:T(8,128)(2,1)S(1)}, bf16[256,3072]{1,0:T(8,128)(2,1)}, bf16[256,3072]{1,0:T(8,128)(2,1)}, bf16[256,3072]{1,0:T(8,128)(2,1)}) custom-call(s32[5]{0:T(128)S(1)} %copy-done.2, s32[48,9]{1,0:T(8,128)S(1)} %copy.10.neighbours_ref, s32[48]{0:T(128)S(1)} %copy-done.3, bf16[1024,1024]{1,0:T(8,128)(2,1)} %order.1.cov_ref, ...), custom_call_target="tpu_custom_call" | custom-call | flops 14495514624 | bytes 19660800 | tf_op jit(solution)/shard_map/products/pallas_call | solution.py:275
  200.6 1.2 copy-done.1
  201.8 0.7 collective-permute-start.16
  202.5 1.6 collective-permute-start.15
  204.1 1.2 copy-done.4
  205.2 3.5 %collective-permute-done.18.refs_2_ = bf16[256,3072]{1,0:T(8,128)(2,1)} collective-permute-done((bf16[256,3072]{1,0:T(8,128)(2,1)}, bf16[256,3072]{1,0:T(8,128)(2,1)}, u32[]{:S(2)}, u32[]{:S(2)}) %collective-permute-start.18) | collective-permute-done | bytes 1572896 | tf_op jit(solution)/shard_map/ppermute | solution.py:380
  208.8 32.8 %collective-permute-done.19.refs_3_ = bf16[256,3072]{1,0:T(8,128)(2,1)} collective-permute-done((bf16[256,3072]{1,0:T(8,128)(2,1)}, bf16[256,3072]{1,0:T(8,128)(2,1)}, u32[]{:S(2)}, u32[]{:S(2)}) %collective-permute-start.19) | collective-permute-done | bytes 1572896 | tf_op jit(solution)/shard_map/ppermute | solution.py:380
  241.6 6.3 %place.4.refs_2_ = bf16[256,24576]{1,0:T(8,128)(2,1)} custom-call(s32[5]{0:T(128)} %pad_add_fusion.place_ref.refs_0_, bf16[256,3072]{1,0:T(8,128)(2,1)} %copy-done, bf16[256,3072]{1,0:T(8,128)(2,1)} %copy-done.4, bf16[256,3072]{1,0:T(8,128)(2,1)} %collective-permute-done.18.refs_2_, bf16[256,3072]{1,0:T(8,128)(2,1)} %collective-permute-done.19.refs_3_), custom_call_target="tpu_custom_call" | custom-call | bytes 12582912 | tf_op jit(solution)/shard_map/place/pallas_call | solution.py:338
  247.9 4.3 %place.5.refs_1_ = bf16[256,24576]{1,0:T(8,128)(2,1)} custom-call(s32[5]{0:T(128)} %pad_add_fusion.place_ref.refs_0_, bf16[256,3072]{1,0:T(8,128)(2,1)} %copy-done.1, bf16[256,3072]{1,0:T(8,128)(2,1)} %collective-permute-done.16.refs_1_, bf16[256,24576]{1,0:T(8,128)(2,1)} %place.4.refs_2_), custom_call_target="tpu_custom_call", output_to_operand_aliasing={{}: (3, {})} | custom-call | bytes 6291456 | tf_op jit(solution)/shard_map/place/pallas_call | solution.py:338
  252.1 23.9 %collective-permute-done.15.refs_0_ = bf16[256,3072]{1,0:T(8,128)(2,1)S(1)} collective-permute-done((bf16[256,3072]{1,0:T(8,128)(2,1)}, bf16[256,3072]{1,0:T(8,128)(2,1)S(1)}, u32[]{:S(2)}, u32[]{:S(2)}) %collective-permute-start.15) | collective-permute-done | bytes 1572896 | tf_op jit(solution)/shard_map/ppermute | solution.py:380
  276.1 1.8 place.6.refs_1_
  277.9 30.8 %collective-permute-done.14.refs_0_ = bf16[256,3072]{1,0:T(8,128)(2,1)S(1)} collective-permute-done((bf16[256,3072]{1,0:T(8,128)(2,1)}, bf16[256,3072]{1,0:T(8,128)(2,1)S(1)}, u32[]{:S(2)}, u32[]{:S(2)}) %collective-permute-start.14) | collective-permute-done | bytes 1572896 | tf_op jit(solution)/shard_map/ppermute | solution.py:380
  308.7 1.8 place.7
  (29 shorter events, 0.1 us)
Async XLA Ops:
  7.6 97.8 %collective-permute-start.5 = (bf16[256,3072]{1,0:T(8,128)(2,1)}, bf16[256,3072]{1,0:T(8,128)(2,1)}, u32[]{:S(2)}, u32[]{:S(2)}) collective-permute-start(bf16[256,3072]{1,0:T(8,128)(2,1)} %get-tuple-element.37), channel_id=1, source_target_pairs={{0,1},{1,0},{2,3},{3,2},{4,5},{5,4},{6,7},{7,6},{8,9},{9,8},{10,11... | collective-permute-start | bytes 4718600 | tf_op jit(solution)/shard_map/ppermute | solution.py:380
  7.7 97.9 %collective-permute-start.6 = (bf16[256,3072]{1,0:T(8,128)(2,1)}, bf16[256,3072]{1,0:T(8,128)(2,1)}, u32[]{:S(2)}, u32[]{:S(2)}) collective-permute-start(bf16[256,3072]{1,0:T(8,128)(2,1)} %get-tuple-element.38), channel_id=1, source_target_pairs={{0,2},{1,3},{2,0},{3,1},{4,6},{5,7},{6,4},{7,5},{8,10},{9,11},{10,... | collective-permute-start | bytes 4718600 | tf_op jit(solution)/shard_map/ppermute | solution.py:380
  9.2 96.3 %collective-permute-start.7 = (bf16[256,3072]{1,0:T(8,128)(2,1)}, bf16[256,3072]{1,0:T(8,128)(2,1)}, u32[]{:S(2)}, u32[]{:S(2)}) collective-permute-start(bf16[256,3072]{1,0:T(8,128)(2,1)} %get-tuple-element.30), channel_id=1, source_target_pairs={{0,3},{1,2},{2,1},{3,0},{4,7},{5,6},{6,5},{7,4},{8,11},{9,10},{10,... | collective-permute-start | bytes 4718600 | tf_op jit(solution)/shard_map/ppermute | solution.py:380
  10.6 16.1 %collective-permute-start.1 = (bf16[256,512]{1,0:T(8,128)(2,1)S(1)}, bf16[256,512]{1,0:T(8,128)(2,1)S(1)}, u32[]{:S(2)}, u32[]{:S(2)}) collective-permute-start(bf16[256,512]{1,0:T(8,128)(2,1)S(1)} %get-tuple-element.51), channel_id=1, source_target_pairs={{4,0},{8,4},{12,8},{16,12},{20,16},{24,20},{28,24},{5,1},{9,5},{13... | collective-permute-start | bytes 786440 | tf_op jit(solution)/shard_map/ppermute | solution.py:394
  13.9 14.3 %collective-permute-start = (bf16[256,512]{1,0:T(8,128)(2,1)S(1)}, bf16[256,512]{1,0:T(8,128)(2,1)S(1)}, u32[]{:S(2)}, u32[]{:S(2)}) collective-permute-start(bf16[256,512]{1,0:T(8,128)(2,1)S(1)} %get-tuple-element.52), channel_id=1, source_target_pairs={{0,4},{4,8},{8,12},{12,16},{16,20},{20,24},{24,28},{1,5},{5,9},{9,... | collective-permute-start | bytes 786440 | tf_op jit(solution)/shard_map/ppermute | solution.py:393
  26.6 2.7 copy-start.5
  26.7 64.3 %copy-start.7 = (s32[48,9]{0,1:T(8,128)S(1)}, s32[48,9]{0,1:T(8,128)}, u32[]{:S(2)}) copy-start(s32[48,9]{0,1:T(8,128)} %param.8) | copy-start | bytes 5188
  26.7 57.9 %collective-permute-start.11 = (bf16[256,512]{1,0:T(8,128)(2,1)S(1)}, bf16[256,512]{1,0:T(8,128)(2,1)S(1)}, u32[]{:S(2)}, u32[]{:S(2)}) collective-permute-start(bf16[256,512]{1,0:T(8,128)(2,1)S(1)} %get-tuple-element.41), channel_id=1, source_target_pairs={{0,2},{1,3},{2,0},{3,1},{4,6},{5,7},{6,4},{7,5},{8,10},{9,11},{10,... | collective-permute-start | bytes 786440 | tf_op jit(solution)/shard_map/ppermute | solution.py:380
  28.2 1.2 copy-start.6
  28.2 60.9 %collective-permute-start.9 = (bf16[256,512]{1,0:T(8,128)(2,1)S(1)}, bf16[256,512]{1,0:T(8,128)(2,1)S(1)}, u32[]{:S(2)}, u32[]{:S(2)}) collective-permute-start(bf16[256,512]{1,0:T(8,128)(2,1)S(1)} %get-tuple-element.28), channel_id=1, source_target_pairs={{0,3},{1,2},{2,1},{3,0},{4,7},{5,6},{6,5},{7,4},{8,11},{9,10},{10,... | collective-permute-start | bytes 786440 | tf_op jit(solution)/shard_map/ppermute | solution.py:380
  84.5 4.9 %collective-permute-start.13 = (bf16[256,512]{1,0:T(8,128)(2,1)S(1)}, bf16[256,512]{1,0:T(8,128)(2,1)S(1)}, u32[]{:S(2)}, u32[]{:S(2)}) collective-permute-start(bf16[256,512]{1,0:T(8,128)(2,1)S(1)} %get-tuple-element.39.refs_4_), channel_id=1, source_target_pairs={{0,1},{1,0},{2,3},{3,2},{4,5},{5,4},{6,7},{7,6},{8,9},{9,8},{10,11... | collective-permute-start | bytes 786440 | tf_op jit(solution)/shard_map/ppermute | solution.py:380
  89.1 1.5 collective-permute-start.8
  89.4 14.2 %collective-permute-start.12 = (bf16[256,512]{1,0:T(8,128)(2,1)S(1)}, bf16[256,512]{1,0:T(8,128)(2,1)S(1)}, u32[]{:S(2)}, u32[]{:S(2)}) collective-permute-start(bf16[256,512]{1,0:T(8,128)(2,1)S(1)} %collective-permute-done.11.refs_10_), channel_id=1, source_target_pairs={{0,1},{1,0},{2,3},{3,2},{4,5},{5,4},{6,7},{7,6},{8,9},{9,8},{10,11... | collective-permute-start | bytes 786440 | tf_op jit(solution)/shard_map/ppermute | solution.py:380
  90.6 13.2 %collective-permute-start.10 = (bf16[256,512]{1,0:T(8,128)(2,1)S(1)}, bf16[256,512]{1,0:T(8,128)(2,1)S(1)}, u32[]{:S(2)}, u32[]{:S(2)}) collective-permute-start(bf16[256,512]{1,0:T(8,128)(2,1)S(1)} %collective-permute-done.9.refs_11_), channel_id=1, source_target_pairs={{0,1},{1,0},{2,3},{3,2},{4,5},{5,4},{6,7},{7,6},{8,9},{9,8},{10,11... | collective-permute-start | bytes 786440 | tf_op jit(solution)/shard_map/ppermute | solution.py:380
  95.5 10.1 %copy-start.2 = (s32[5]{0:T(128)S(1)}, s32[5]{0:T(128)}, u32[]{:S(2)}) copy-start(s32[5]{0:T(128)} %pad_add_fusion.place_ref.refs_0_) | copy-start | bytes 64
  95.5 10.1 %copy-start.3 = (s32[48]{0:T(128)S(1)}, s32[48]{0:T(128)}, u32[]{:S(2)}) copy-start(s32[48]{0:T(128)} %counts_ref.3) | copy-start | bytes 580
  103.6 33.5 %collective-permute-start.2 = (bf16[256,3072]{1,0:T(8,128)(2,1)}, bf16[256,3072]{1,0:T(8,128)(2,1)S(1)}, u32[]{:S(2)}, u32[]{:S(2)}) collective-permute-start(bf16[256,3072]{1,0:T(8,128)(2,1)} %get-tuple-element.33), channel_id=1, source_target_pairs={{0,1},{1,0},{2,3},{3,2},{4,5},{5,4},{6,7},{7,6},{8,9},{9,8},{10,11... | collective-permute-start | bytes 4718600 | tf_op jit(solution)/shard_map/ppermute | solution.py:380
  103.7 37.5 %collective-permute-start.3 = (bf16[256,3072]{1,0:T(8,128)(2,1)}, bf16[256,3072]{1,0:T(8,128)(2,1)S(1)}, u32[]{:S(2)}, u32[]{:S(2)}) collective-permute-start(bf16[256,3072]{1,0:T(8,128)(2,1)} %get-tuple-element.34), channel_id=1, source_target_pairs={{0,2},{1,3},{2,0},{3,1},{4,6},{5,7},{6,4},{7,5},{8,10},{9,11},{10,... | collective-permute-start | bytes 4718600 | tf_op jit(solution)/shard_map/ppermute | solution.py:380
  105.3 68.8 %collective-permute-start.4 = (bf16[256,3072]{1,0:T(8,128)(2,1)}, bf16[256,3072]{1,0:T(8,128)(2,1)S(1)}, u32[]{:S(2)}, u32[]{:S(2)}) collective-permute-start(bf16[256,3072]{1,0:T(8,128)(2,1)} %get-tuple-element.35), channel_id=1, source_target_pairs={{0,3},{1,2},{2,1},{3,0},{4,7},{5,6},{6,5},{7,4},{8,11},{9,10},{10,... | collective-permute-start | bytes 4718600 | tf_op jit(solution)/shard_map/ppermute | solution.py:380
  133.9 1.2 copy-start
  135.1 69.0 %collective-permute-start.17 = (bf16[256,3072]{1,0:T(8,128)(2,1)S(1)}, bf16[256,3072]{1,0:T(8,128)(2,1)S(1)}, u32[]{:S(2)}, u32[]{:S(2)}) collective-permute-start(bf16[256,3072]{1,0:T(8,128)(2,1)S(1)} %get-tuple-element.48), channel_id=1, source_target_pairs={{0,1},{1,0},{2,3},{3,2},{4,5},{5,4},{6,7},{7,6},{8,9},{9,8},{10,11... | collective-permute-start | bytes 4718600 | tf_op jit(solution)/shard_map/ppermute | solution.py:380
  135.5 73.3 %collective-permute-start.18 = (bf16[256,3072]{1,0:T(8,128)(2,1)}, bf16[256,3072]{1,0:T(8,128)(2,1)}, u32[]{:S(2)}, u32[]{:S(2)}) collective-permute-start(bf16[256,3072]{1,0:T(8,128)(2,1)} %get-tuple-element.49), channel_id=1, source_target_pairs={{0,2},{1,3},{2,0},{3,1},{4,6},{5,7},{6,4},{7,5},{8,10},{9,11},{10,... | collective-permute-start | bytes 4718600 | tf_op jit(solution)/shard_map/ppermute | solution.py:380
  137.1 37.1 %copy-start.8 = (bf16[256,3072]{1,0:T(8,128)(2,1)}, bf16[256,3072]{1,0:T(8,128)(2,1)S(1)}, u32[]{:S(2)}) copy-start(bf16[256,3072]{1,0:T(8,128)(2,1)S(1)} %collective-permute-done.2.refs_1_) | copy-start | bytes 4718596
  137.1 104.5 %collective-permute-start.19 = (bf16[256,3072]{1,0:T(8,128)(2,1)}, bf16[256,3072]{1,0:T(8,128)(2,1)}, u32[]{:S(2)}, u32[]{:S(2)}) collective-permute-start(bf16[256,3072]{1,0:T(8,128)(2,1)} %get-tuple-element.50), channel_id=1, source_target_pairs={{0,3},{1,2},{2,1},{3,0},{4,7},{5,6},{6,5},{7,4},{8,11},{9,10},{10,... | collective-permute-start | bytes 4718600 | tf_op jit(solution)/shard_map/ppermute | solution.py:380
  141.2 32.9 %copy-start.9 = (bf16[256,3072]{1,0:T(8,128)(2,1)}, bf16[256,3072]{1,0:T(8,128)(2,1)S(1)}, u32[]{:S(2)}) copy-start(bf16[256,3072]{1,0:T(8,128)(2,1)S(1)} %collective-permute-done.3.refs_2_) | copy-start | bytes 4718596
  174.2 1.2 copy-start.10
  200.6 1.2 copy-start.1
  201.8 46.0 %collective-permute-start.16 = (bf16[256,3072]{1,0:T(8,128)(2,1)}, bf16[256,3072]{1,0:T(8,128)(2,1)}, u32[]{:S(2)}, u32[]{:S(2)}) collective-permute-start(bf16[256,3072]{1,0:T(8,128)(2,1)} %get-tuple-element.46), channel_id=1, source_target_pairs={{0,1},{1,0},{2,3},{3,2},{4,5},{5,4},{6,7},{7,6},{8,9},{9,8},{10,11... | collective-permute-start | bytes 4718600 | tf_op jit(solution)/shard_map/ppermute | solution.py:380
  202.5 73.6 %collective-permute-start.15 = (bf16[256,3072]{1,0:T(8,128)(2,1)}, bf16[256,3072]{1,0:T(8,128)(2,1)S(1)}, u32[]{:S(2)}, u32[]{:S(2)}) collective-permute-start(bf16[256,3072]{1,0:T(8,128)(2,1)} %get-tuple-element.44), channel_id=1, source_target_pairs={{0,2},{1,3},{2,0},{3,1},{4,6},{5,7},{6,4},{7,5},{8,10},{9,11},{10,... | collective-permute-start | bytes 4718600 | tf_op jit(solution)/shard_map/ppermute | solution.py:380
  204.1 1.2 copy-start.4
  205.2 103.4 %collective-permute-start.14 = (bf16[256,3072]{1,0:T(8,128)(2,1)}, bf16[256,3072]{1,0:T(8,128)(2,1)S(1)}, u32[]{:S(2)}, u32[]{:S(2)}) collective-permute-start(bf16[256,3072]{1,0:T(8,128)(2,1)} %get-tuple-element.43), channel_id=1, source_target_pairs={{0,3},{1,2},{2,1},{3,0},{4,7},{5,6},{6,5},{7,4},{8,11},{9,10},{10,... | collective-permute-start | bytes 4718600 | tf_op jit(solution)/shard_map/ppermute | solution.py:380

commit v3 on v2

--- a/solution.py
+++ b/solution.py
@@ -298,8 +298,13 @@
     return results[:groups], (results[groups] if has_next else None)
 
 
-def place_kernel(peers, chunks, chunk, place_ref, *refs):
+def place_kernel(peers, chunks, chunk, on_chip, *refs):
     target, sems = refs[-2], refs[-1]
+    if on_chip:
+        mine = lax.axis_index("tm")
+        place_ref = {peer: jnp.bitwise_xor(mine, peer) for peer in peers}
+    else:
+        place_ref, *refs = refs
     copies = []
     for which, peer in enumerate(peers):
         source = refs[which]
@@ -328,18 +333,19 @@
     hours_dev, columns = pieces[0].shape
     in_specs = [pl.BlockSpec(memory_space=pltpu.VMEM)] * len(pieces)
     operands = list(pieces)
+    scalars = [] if on_chip else [place]
     if on_chip:
         operands = [pltpu.with_memory_space_constraint(piece, pltpu.VMEM) for piece in pieces]
     aliases = {}
     if result is not None:
         in_specs += [pl.BlockSpec(memory_space=pl.ANY)]
         operands += [result]
-        aliases = {1 + len(pieces): 0}
+        aliases = {len(scalars) + len(pieces): 0}
     return pl.pallas_call(
-        functools.partial(place_kernel, peers, chunks, chunk),
+        functools.partial(place_kernel, peers, chunks, chunk, on_chip),
         out_shape=jax.ShapeDtypeStruct((hours_dev, cells_dev), pieces[0].dtype),
         grid_spec=pltpu.PrefetchScalarGridSpec(
-            num_scalar_prefetch=1,
+            num_scalar_prefetch=len(scalars),
             grid=(),
             in_specs=in_specs,
             out_specs=pl.BlockSpec(memory_space=pl.ANY),
@@ -350,7 +356,7 @@
             flops=0, transcendentals=0, bytes_accessed=4 * len(pieces) * hours_dev * columns
         ),
         name="place",
-    )(place, *operands)
+    )(*scalars, *operands)
 
 
 def per_device(field, temporal_cov, spatial_blocks, neighbours, counts):

time: 312 us -> 312 us (level)
  no operation moved by 1% of the time
where the time goes in v3:
time: 312 us; the launch traced here: 310 us
  waiting for transfers between devices  200 us (64%)
  Pallas kernels  87.1 us (28%)
  starting transfers between devices  16.3 us (5%)
  local copies, waits for them, and re-layouts  5.91 us (2%)
    ppermute x18, waiting for transfers between devices, swap(): return lax.ppermute(array, 'tm', [(at, at ^ peer) for at in range(groups)])  189 us
    pallas_call x2, Pallas kernels, products(): pl.pallas_call(functools.partial(product_kernel, cfg), out_shape=out_shap...  53.6 us
    pallas_call x4, Pallas kernels, put(): pl.pallas_call(functools.partial(place_kernel, peers, chunks, chunk, on_c...  12.9 us
    ppermute x18, starting transfers between devices, swap(): return lax.ppermute(array, 'tm', [(at, at ^ peer) for at in range(groups)])  10.4 us
    ppermute x1, waiting for transfers between devices, per_device(): high = lax.ppermute(field[:, :unit], 'space', backward)  10.2 us
    pallas_call x1, Pallas kernels, pack(): pl.pallas_call(functools.partial(pack_kernel, last, sources), out_shape=[...  8.1 us
    pallas_call x3, Pallas kernels, pack(): pl.pallas_call(functools.partial(copy_kernel, unit, sources, peers, on_ch...  8.07 us
  transfers between devices with their start and end apart: 20, of which 10 were waited for; matrix products, arithmetic and copies ran while one was open for 0% of the time, Pallas kernels for 26%

profile of v3, /device:TPU:16, one launch (start us, length us, event | category | flops | bytes accessed | tf_op | source)
XLA Modules:
  0.0 309.8 jit_solution(11315766074869537786)
XLA Ops:
  0.0 1.1 pack.4
  1.1 0.6 pad_add_fusion.place_ref.refs_0_
  1.7 5.8 %pack.5 = (bf16[256,3072]{1,0:T(8,128)(2,1)}, bf16[256,3072]{1,0:T(8,128)(2,1)}, bf16[256,3072]{1,0:T(8,128)(2,1)}, bf16[256,3072]{1,0:T(8,128)(2,1)}) custom-call(s32[5]{0:T(128)} %pad_add_fusion.place_ref.refs_0_, bf16[256,24576]{1,0:T(8,128)(2,1)} %refs_0_.5), custom_call_target="tpu_custom_call" | custom-call | bytes 12582912 | tf_op jit(solution)/shard_map/pack/pallas_call | solution.py:89
  7.6 0.1 collective-permute-start.5
  7.7 1.6 collective-permute-start.6
  9.2 0.3 collective-permute-start.7
  9.5 1.1 fusion
  10.6 3.3 %collective-permute-start.1 = (bf16[256,512]{1,0:T(8,128)(2,1)S(1)}, bf16[256,512]{1,0:T(8,128)(2,1)S(1)}, u32[]{:S(2)}, u32[]{:S(2)}) collective-permute-start(bf16[256,512]{1,0:T(8,128)(2,1)S(1)} %get-tuple-element.51), channel_id=1, source_target_pairs={{4,0},{8,4},{12,8},{16,12},{20,16},{24,20},{28,24},{5,1},{9,5},{13... | collective-permute-start | bytes 786440 | tf_op jit(solution)/shard_map/ppermute | solution.py:400
  13.9 2.6 collective-permute-start
  16.4 10.2 %collective-permute-done.1.refs_5_ = bf16[256,512]{1,0:T(8,128)(2,1)S(1)} collective-permute-done((bf16[256,512]{1,0:T(8,128)(2,1)S(1)}, bf16[256,512]{1,0:T(8,128)(2,1)S(1)}, u32[]{:S(2)}, u32[]{:S(2)}) %collective-permute-start.1) | collective-permute-done | bytes 262176 | tf_op jit(solution)/shard_map/ppermute | solution.py:400
  26.7 1.5 collective-permute-start.11
  28.2 0.0 collective-permute-done.refs_4_
  28.2 0.0 collective-permute-start.9
  28.2 1.2 pack.7
  29.4 55.1 %collective-permute-done.11.refs_10_ = bf16[256,512]{1,0:T(8,128)(2,1)S(1)} collective-permute-done((bf16[256,512]{1,0:T(8,128)(2,1)S(1)}, bf16[256,512]{1,0:T(8,128)(2,1)S(1)}, u32[]{:S(2)}, u32[]{:S(2)}) %collective-permute-start.11) | collective-permute-done | bytes 262176 | tf_op jit(solution)/shard_map/ppermute | solution.py:386
  84.5 4.5 %collective-permute-done.9.refs_11_ = bf16[256,512]{1,0:T(8,128)(2,1)S(1)} collective-permute-done((bf16[256,512]{1,0:T(8,128)(2,1)S(1)}, bf16[256,512]{1,0:T(8,128)(2,1)S(1)}, u32[]{:S(2)}, u32[]{:S(2)}) %collective-permute-start.9) | collective-permute-done | bytes 262176 | tf_op jit(solution)/shard_map/ppermute | solution.py:386
  89.1 0.4 collective-permute-start.8
  89.4 0.0 collective-permute-done.13.refs_9_
  89.4 0.1 collective-permute-start.12
  89.6 1.0 collective-permute-done.8.refs_5_
  90.6 0.4 collective-permute-start.10
  91.0 0.1 copy.10.neighbours_ref
  91.0 4.5 %order.1.cov_ref = bf16[1024,1024]{1,0:T(8,128)(2,1)} custom-call(s32[5]{0:T(128)} %pad_add_fusion.place_ref.refs_0_, bf16[1024,1024]{1,0:T(8,128)(2,1)} %source.1), custom_call_target="tpu_custom_call" | custom-call | tf_op jit(solution)/shard_map/order/pallas_call | solution.py:133
  95.5 8.1 %pack.6 = (bf16[256,3072]{1,0:T(8,128)(2,1)}, bf16[256,3072]{1,0:T(8,128)(2,1)}, bf16[256,3072]{1,0:T(8,128)(2,1)}, bf16[256,3072]{1,0:T(8,128)(2,1)}) custom-call(s32[5]{0:T(128)} %pad_add_fusion.place_ref.refs_0_, bf16[256,24576]{1,0:T(8,128)(2,1)} %refs_0_.5, bf16[256,24576]{1,0:T(8,128)(2,1)} %refs_0_.5, bf16[256,24576]{1,0:T(8,128)(2,1)} %refs_0_.5, ...), custom_call_target="tpu_custom_call" | custom-call | bytes 12582912 | tf_op jit(solution)/shard_map/pack/pallas_call | solution.py:108
  103.6 0.1 collective-permute-start.2
  103.7 0.0 collective-permute-done.10.refs_6_
  103.7 1.6 collective-permute-start.3
  105.3 0.2 collective-permute-start.4
  105.6 28.3 %products.2 = (bf16[256,3072]{1,0:T(8,128)(2,1)S(1)}, bf16[256,3072]{1,0:T(8,128)(2,1)S(1)}, bf16[256,3072]{1,0:T(8,128)(2,1)}, bf16[256,3072]{1,0:T(8,128)(2,1)}, bf16[1024,1024]{1,0:T(8,128)(2,1)}) custom-call(s32[5]{0:T(128)S(1)} %copy-done.2, s32[48,9]{1,0:T(8,128)S(1)} %copy.10.neighbours_ref, s32[48]{0:T(128)S(1)} %copy-done.3, ...), custom_call_target="tpu_custom_call" | custom-call | flops 16642998272 | bytes 21757952 | tf_op jit(solution)/shard_map/products/pallas_call | solution.py:275
  133.9 1.2 copy-done
  135.1 0.4 collective-permute-start.17
  135.5 1.6 collective-permute-start.18
  137.1 4.2 %collective-permute-done.3.refs_2_ = bf16[256,3072]{1,0:T(8,128)(2,1)S(1)} collective-permute-done((bf16[256,3072]{1,0:T(8,128)(2,1)}, bf16[256,3072]{1,0:T(8,128)(2,1)S(1)}, u32[]{:S(2)}, u32[]{:S(2)}) %collective-permute-start.3) | collective-permute-done | bytes 1572896 | tf_op jit(solution)/shard_map/ppermute | solution.py:386
  141.2 32.9 %collective-permute-done.4.refs_3_ = bf16[256,3072]{1,0:T(8,128)(2,1)S(1)} collective-permute-done((bf16[256,3072]{1,0:T(8,128)(2,1)}, bf16[256,3072]{1,0:T(8,128)(2,1)S(1)}, u32[]{:S(2)}, u32[]{:S(2)}) %collective-permute-start.4) | collective-permute-done | bytes 1572896 | tf_op jit(solution)/shard_map/ppermute | solution.py:386
  174.2 1.2 copy-done.10
  175.3 25.3 %products.3 = (bf16[256,3072]{1,0:T(8,128)(2,1)S(1)}, bf16[256,3072]{1,0:T(8,128)(2,1)}, bf16[256,3072]{1,0:T(8,128)(2,1)}, bf16[256,3072]{1,0:T(8,128)(2,1)}) custom-call(s32[5]{0:T(128)S(1)} %copy-done.2, s32[48,9]{1,0:T(8,128)S(1)} %copy.10.neighbours_ref, s32[48]{0:T(128)S(1)} %copy-done.3, bf16[1024,1024]{1,0:T(8,128)(2,1)} %order.1.cov_ref, ...), custom_call_target="tpu_custom_call" | custom-call | flops 14495514624 | bytes 19660800 | tf_op jit(solution)/shard_map/products/pallas_call | solution.py:275
  200.6 1.2 copy-done.1
  201.8 0.7 collective-permute-start.16
  202.5 1.6 collective-permute-start.15
  204.1 1.2 copy-done.4
  205.2 3.5 %collective-permute-done.18.refs_3_ = bf16[256,3072]{1,0:T(8,128)(2,1)} collective-permute-done((bf16[256,3072]{1,0:T(8,128)(2,1)}, bf16[256,3072]{1,0:T(8,128)(2,1)}, u32[]{:S(2)}, u32[]{:S(2)}) %collective-permute-start.18) | collective-permute-done | bytes 1572896 | tf_op jit(solution)/shard_map/ppermute | solution.py:386
  208.8 32.8 %collective-permute-done.19.refs_4_ = bf16[256,3072]{1,0:T(8,128)(2,1)} collective-permute-done((bf16[256,3072]{1,0:T(8,128)(2,1)}, bf16[256,3072]{1,0:T(8,128)(2,1)}, u32[]{:S(2)}, u32[]{:S(2)}) %collective-permute-start.19) | collective-permute-done | bytes 1572896 | tf_op jit(solution)/shard_map/ppermute | solution.py:386
  241.6 6.3 %place.4.refs_3_ = bf16[256,24576]{1,0:T(8,128)(2,1)} custom-call(s32[5]{0:T(128)} %pad_add_fusion.place_ref.refs_0_, bf16[256,3072]{1,0:T(8,128)(2,1)} %copy-done, bf16[256,3072]{1,0:T(8,128)(2,1)} %copy-done.4, bf16[256,3072]{1,0:T(8,128)(2,1)} %collective-permute-done.18.refs_3_, bf16[256,3072]{1,0:T(8,128)(2,1)} %collective-permute-done.19.refs_4_), custom_call_target="tpu_custom_call" | custom-call | bytes 12582912 | tf_op jit(solution)/shard_map/place/pallas_call | solution.py:344
  247.9 4.3 %place.5.refs_1_ = bf16[256,24576]{1,0:T(8,128)(2,1)} custom-call(s32[5]{0:T(128)} %pad_add_fusion.place_ref.refs_0_, bf16[256,3072]{1,0:T(8,128)(2,1)} %copy-done.1, bf16[256,3072]{1,0:T(8,128)(2,1)} %collective-permute-done.16.refs_2_, bf16[256,24576]{1,0:T(8,128)(2,1)} %place.4.refs_3_), custom_call_target="tpu_custom_call", output_to_operand_aliasing={{}: (3, {})} | custom-call | bytes 6291456 | tf_op jit(solution)/shard_map/place/pallas_call | solution.py:344
  252.1 23.9 %collective-permute-done.15.refs_0_ = bf16[256,3072]{1,0:T(8,128)(2,1)S(1)} collective-permute-done((bf16[256,3072]{1,0:T(8,128)(2,1)}, bf16[256,3072]{1,0:T(8,128)(2,1)S(1)}, u32[]{:S(2)}, u32[]{:S(2)}) %collective-permute-start.15) | collective-permute-done | bytes 1572896 | tf_op jit(solution)/shard_map/ppermute | solution.py:386
  276.1 1.2 place.6.refs_1_
  277.2 31.4 %collective-permute-done.14.refs_0_ = bf16[256,3072]{1,0:T(8,128)(2,1)S(1)} collective-permute-done((bf16[256,3072]{1,0:T(8,128)(2,1)}, bf16[256,3072]{1,0:T(8,128)(2,1)S(1)}, u32[]{:S(2)}, u32[]{:S(2)}) %collective-permute-start.14) | collective-permute-done | bytes 1572896 | tf_op jit(solution)/shard_map/ppermute | solution.py:386
  308.7 1.2 place.7
  (29 shorter events, 0.1 us)
Async XLA Ops:
  7.6 97.8 %collective-permute-start.5 = (bf16[256,3072]{1,0:T(8,128)(2,1)}, bf16[256,3072]{1,0:T(8,128)(2,1)}, u32[]{:S(2)}, u32[]{:S(2)}) collective-permute-start(bf16[256,3072]{1,0:T(8,128)(2,1)} %get-tuple-element.37), channel_id=1, source_target_pairs={{0,1},{1,0},{2,3},{3,2},{4,5},{5,4},{6,7},{7,6},{8,9},{9,8},{10,11... | collective-permute-start | bytes 4718600 | tf_op jit(solution)/shard_map/ppermute | solution.py:386
  7.7 97.9 %collective-permute-start.6 = (bf16[256,3072]{1,0:T(8,128)(2,1)}, bf16[256,3072]{1,0:T(8,128)(2,1)}, u32[]{:S(2)}, u32[]{:S(2)}) collective-permute-start(bf16[256,3072]{1,0:T(8,128)(2,1)} %get-tuple-element.38), channel_id=1, source_target_pairs={{0,2},{1,3},{2,0},{3,1},{4,6},{5,7},{6,4},{7,5},{8,10},{9,11},{10,... | collective-permute-start | bytes 4718600 | tf_op jit(solution)/shard_map/ppermute | solution.py:386
  9.2 96.3 %collective-permute-start.7 = (bf16[256,3072]{1,0:T(8,128)(2,1)}, bf16[256,3072]{1,0:T(8,128)(2,1)}, u32[]{:S(2)}, u32[]{:S(2)}) collective-permute-start(bf16[256,3072]{1,0:T(8,128)(2,1)} %get-tuple-element.30), channel_id=1, source_target_pairs={{0,3},{1,2},{2,1},{3,0},{4,7},{5,6},{6,5},{7,4},{8,11},{9,10},{10,... | collective-permute-start | bytes 4718600 | tf_op jit(solution)/shard_map/ppermute | solution.py:386
  10.6 16.1 %collective-permute-start.1 = (bf16[256,512]{1,0:T(8,128)(2,1)S(1)}, bf16[256,512]{1,0:T(8,128)(2,1)S(1)}, u32[]{:S(2)}, u32[]{:S(2)}) collective-permute-start(bf16[256,512]{1,0:T(8,128)(2,1)S(1)} %get-tuple-element.51), channel_id=1, source_target_pairs={{4,0},{8,4},{12,8},{16,12},{20,16},{24,20},{28,24},{5,1},{9,5},{13... | collective-permute-start | bytes 786440 | tf_op jit(solution)/shard_map/ppermute | solution.py:400
  13.9 14.3 %collective-permute-start = (bf16[256,512]{1,0:T(8,128)(2,1)S(1)}, bf16[256,512]{1,0:T(8,128)(2,1)S(1)}, u32[]{:S(2)}, u32[]{:S(2)}) collective-permute-start(bf16[256,512]{1,0:T(8,128)(2,1)S(1)} %get-tuple-element.52), channel_id=1, source_target_pairs={{0,4},{4,8},{8,12},{12,16},{16,20},{20,24},{24,28},{1,5},{5,9},{9,... | collective-permute-start | bytes 786440 | tf_op jit(solution)/shard_map/ppermute | solution.py:399
  26.6 2.7 copy-start.5
  26.7 64.3 %copy-start.7 = (s32[48,9]{0,1:T(8,128)S(1)}, s32[48,9]{0,1:T(8,128)}, u32[]{:S(2)}) copy-start(s32[48,9]{0,1:T(8,128)} %param.8) | copy-start | bytes 5188
  26.7 57.9 %collective-permute-start.11 = (bf16[256,512]{1,0:T(8,128)(2,1)S(1)}, bf16[256,512]{1,0:T(8,128)(2,1)S(1)}, u32[]{:S(2)}, u32[]{:S(2)}) collective-permute-start(bf16[256,512]{1,0:T(8,128)(2,1)S(1)} %get-tuple-element.41), channel_id=1, source_target_pairs={{0,2},{1,3},{2,0},{3,1},{4,6},{5,7},{6,4},{7,5},{8,10},{9,11},{10,... | collective-permute-start | bytes 786440 | tf_op jit(solution)/shard_map/ppermute | solution.py:386
  28.2 1.2 copy-start.6
  28.2 60.9 %collective-permute-start.9 = (bf16[256,512]{1,0:T(8,128)(2,1)S(1)}, bf16[256,512]{1,0:T(8,128)(2,1)S(1)}, u32[]{:S(2)}, u32[]{:S(2)}) collective-permute-start(bf16[256,512]{1,0:T(8,128)(2,1)S(1)} %get-tuple-element.28), channel_id=1, source_target_pairs={{0,3},{1,2},{2,1},{3,0},{4,7},{5,6},{6,5},{7,4},{8,11},{9,10},{10,... | collective-permute-start | bytes 786440 | tf_op jit(solution)/shard_map/ppermute | solution.py:386
  84.5 4.9 %collective-permute-start.13 = (bf16[256,512]{1,0:T(8,128)(2,1)S(1)}, bf16[256,512]{1,0:T(8,128)(2,1)S(1)}, u32[]{:S(2)}, u32[]{:S(2)}) collective-permute-start(bf16[256,512]{1,0:T(8,128)(2,1)S(1)} %get-tuple-element.39.refs_4_), channel_id=1, source_target_pairs={{0,1},{1,0},{2,3},{3,2},{4,5},{5,4},{6,7},{7,6},{8,9},{9,8},{10,11... | collective-permute-start | bytes 786440 | tf_op jit(solution)/shard_map/ppermute | solution.py:386
  89.1 1.5 collective-permute-start.8
  89.4 14.2 %collective-permute-start.12 = (bf16[256,512]{1,0:T(8,128)(2,1)S(1)}, bf16[256,512]{1,0:T(8,128)(2,1)S(1)}, u32[]{:S(2)}, u32[]{:S(2)}) collective-permute-start(bf16[256,512]{1,0:T(8,128)(2,1)S(1)} %collective-permute-done.11.refs_10_), channel_id=1, source_target_pairs={{0,1},{1,0},{2,3},{3,2},{4,5},{5,4},{6,7},{7,6},{8,9},{9,8},{10,11... | collective-permute-start | bytes 786440 | tf_op jit(solution)/shard_map/ppermute | solution.py:386
  90.6 13.2 %collective-permute-start.10 = (bf16[256,512]{1,0:T(8,128)(2,1)S(1)}, bf16[256,512]{1,0:T(8,128)(2,1)S(1)}, u32[]{:S(2)}, u32[]{:S(2)}) collective-permute-start(bf16[256,512]{1,0:T(8,128)(2,1)S(1)} %collective-permute-done.9.refs_11_), channel_id=1, source_target_pairs={{0,1},{1,0},{2,3},{3,2},{4,5},{5,4},{6,7},{7,6},{8,9},{9,8},{10,11... | collective-permute-start | bytes 786440 | tf_op jit(solution)/shard_map/ppermute | solution.py:386
  95.5 10.1 %copy-start.2 = (s32[5]{0:T(128)S(1)}, s32[5]{0:T(128)}, u32[]{:S(2)}) copy-start(s32[5]{0:T(128)} %pad_add_fusion.place_ref.refs_0_) | copy-start | bytes 64
  95.5 10.1 %copy-start.3 = (s32[48]{0:T(128)S(1)}, s32[48]{0:T(128)}, u32[]{:S(2)}) copy-start(s32[48]{0:T(128)} %counts_ref.3) | copy-start | bytes 580
  103.6 33.5 %collective-permute-start.2 = (bf16[256,3072]{1,0:T(8,128)(2,1)}, bf16[256,3072]{1,0:T(8,128)(2,1)S(1)}, u32[]{:S(2)}, u32[]{:S(2)}) collective-permute-start(bf16[256,3072]{1,0:T(8,128)(2,1)} %get-tuple-element.33), channel_id=1, source_target_pairs={{0,1},{1,0},{2,3},{3,2},{4,5},{5,4},{6,7},{7,6},{8,9},{9,8},{10,11... | collective-permute-start | bytes 4718600 | tf_op jit(solution)/shard_map/ppermute | solution.py:386
  103.7 37.5 %collective-permute-start.3 = (bf16[256,3072]{1,0:T(8,128)(2,1)}, bf16[256,3072]{1,0:T(8,128)(2,1)S(1)}, u32[]{:S(2)}, u32[]{:S(2)}) collective-permute-start(bf16[256,3072]{1,0:T(8,128)(2,1)} %get-tuple-element.34), channel_id=1, source_target_pairs={{0,2},{1,3},{2,0},{3,1},{4,6},{5,7},{6,4},{7,5},{8,10},{9,11},{10,... | collective-permute-start | bytes 4718600 | tf_op jit(solution)/shard_map/ppermute | solution.py:386
  105.3 68.8 %collective-permute-start.4 = (bf16[256,3072]{1,0:T(8,128)(2,1)}, bf16[256,3072]{1,0:T(8,128)(2,1)S(1)}, u32[]{:S(2)}, u32[]{:S(2)}) collective-permute-start(bf16[256,3072]{1,0:T(8,128)(2,1)} %get-tuple-element.35), channel_id=1, source_target_pairs={{0,3},{1,2},{2,1},{3,0},{4,7},{5,6},{6,5},{7,4},{8,11},{9,10},{10,... | collective-permute-start | bytes 4718600 | tf_op jit(solution)/shard_map/ppermute | solution.py:386
  133.9 1.2 copy-start
  135.1 69.0 %collective-permute-start.17 = (bf16[256,3072]{1,0:T(8,128)(2,1)S(1)}, bf16[256,3072]{1,0:T(8,128)(2,1)S(1)}, u32[]{:S(2)}, u32[]{:S(2)}) collective-permute-start(bf16[256,3072]{1,0:T(8,128)(2,1)S(1)} %get-tuple-element.48), channel_id=1, source_target_pairs={{0,1},{1,0},{2,3},{3,2},{4,5},{5,4},{6,7},{7,6},{8,9},{9,8},{10,11... | collective-permute-start | bytes 4718600 | tf_op jit(solution)/shard_map/ppermute | solution.py:386
  135.5 73.3 %collective-permute-start.18 = (bf16[256,3072]{1,0:T(8,128)(2,1)}, bf16[256,3072]{1,0:T(8,128)(2,1)}, u32[]{:S(2)}, u32[]{:S(2)}) collective-permute-start(bf16[256,3072]{1,0:T(8,128)(2,1)} %get-tuple-element.49), channel_id=1, source_target_pairs={{0,2},{1,3},{2,0},{3,1},{4,6},{5,7},{6,4},{7,5},{8,10},{9,11},{10,... | collective-permute-start | bytes 4718600 | tf_op jit(solution)/shard_map/ppermute | solution.py:386
  137.1 37.1 %copy-start.8 = (bf16[256,3072]{1,0:T(8,128)(2,1)}, bf16[256,3072]{1,0:T(8,128)(2,1)S(1)}, u32[]{:S(2)}) copy-start(bf16[256,3072]{1,0:T(8,128)(2,1)S(1)} %collective-permute-done.2.refs_1_) | copy-start | bytes 4718596
  137.1 104.5 %collective-permute-start.19 = (bf16[256,3072]{1,0:T(8,128)(2,1)}, bf16[256,3072]{1,0:T(8,128)(2,1)}, u32[]{:S(2)}, u32[]{:S(2)}) collective-permute-start(bf16[256,3072]{1,0:T(8,128)(2,1)} %get-tuple-element.50), channel_id=1, source_target_pairs={{0,3},{1,2},{2,1},{3,0},{4,7},{5,6},{6,5},{7,4},{8,11},{9,10},{10,... | collective-permute-start | bytes 4718600 | tf_op jit(solution)/shard_map/ppermute | solution.py:386
  141.2 32.9 %copy-start.9 = (bf16[256,3072]{1,0:T(8,128)(2,1)}, bf16[256,3072]{1,0:T(8,128)(2,1)S(1)}, u32[]{:S(2)}) copy-start(bf16[256,3072]{1,0:T(8,128)(2,1)S(1)} %collective-permute-done.3.refs_2_) | copy-start | bytes 4718596
  174.2 1.2 copy-start.10
  200.6 1.2 copy-start.1
  201.8 46.0 %collective-permute-start.16 = (bf16[256,3072]{1,0:T(8,128)(2,1)}, bf16[256,3072]{1,0:T(8,128)(2,1)}, u32[]{:S(2)}, u32[]{:S(2)}) collective-permute-start(bf16[256,3072]{1,0:T(8,128)(2,1)} %get-tuple-element.46), channel_id=1, source_target_pairs={{0,1},{1,0},{2,3},{3,2},{4,5},{5,4},{6,7},{7,6},{8,9},{9,8},{10,11... | collective-permute-start | bytes 4718600 | tf_op jit(solution)/shard_map/ppermute | solution.py:386
  202.5 73.6 %collective-permute-start.15 = (bf16[256,3072]{1,0:T(8,128)(2,1)}, bf16[256,3072]{1,0:T(8,128)(2,1)S(1)}, u32[]{:S(2)}, u32[]{:S(2)}) collective-permute-start(bf16[256,3072]{1,0:T(8,128)(2,1)} %get-tuple-element.44), channel_id=1, source_target_pairs={{0,2},{1,3},{2,0},{3,1},{4,6},{5,7},{6,4},{7,5},{8,10},{9,11},{10,... | collective-permute-start | bytes 4718600 | tf_op jit(solution)/shard_map/ppermute | solution.py:386
  204.1 1.2 copy-start.4
  205.2 103.4 %collective-permute-start.14 = (bf16[256,3072]{1,0:T(8,128)(2,1)}, bf16[256,3072]{1,0:T(8,128)(2,1)S(1)}, u32[]{:S(2)}, u32[]{:S(2)}) collective-permute-start(bf16[256,3072]{1,0:T(8,128)(2,1)} %get-tuple-element.43), channel_id=1, source_target_pairs={{0,3},{1,2},{2,1},{3,0},{4,7},{5,6},{6,5},{7,4},{8,11},{9,10},{10,... | collective-permute-start | bytes 4718600 | tf_op jit(solution)/shard_map/ppermute | solution.py:386

commit v4 on v3

--- a/solution.py
+++ b/solution.py
@@ -153,6 +153,7 @@
     carry_ref = None if opening else refs.pop(0)
     tiles_ref = refs.pop(0)
     outs = [refs.pop(0) for _ in range(groups)]
+    final_ref = None if has_next else refs.pop(0)
     next_ref = refs.pop(0) if has_next else None
     panel, mixed, banded = refs
 
@@ -224,9 +225,17 @@
                 window, banded[pair], (((1,), (1,)), ((), ())), preferred_element_type=jnp.float32
             ).astype(outs[0].dtype)
             for peer in range(groups):
-                outs[peer][:, 2 * pair * block : 2 * (pair + 1) * block] = summed[
-                    peer * hours_dev : (peer + 1) * hours_dev
-                ]
+
+                def store(target):
+                    target[:, 2 * pair * block : 2 * (pair + 1) * block] = summed[
+                        peer * hours_dev : (peer + 1) * hours_dev
+                    ]
+
+                if final_ref is not None and peer == groups - 1:
+                    pl.when(turn < chunk_units - 1)(lambda: store(outs[-1]))
+                    pl.when(turn == chunk_units - 1)(lambda: store(final_ref))
+                else:
+                    store(outs[peer])
 
 
 def products(place, neighbours, counts, cov, pieces, start, carry, spatial_blocks, layout, chunk):
@@ -264,6 +273,19 @@
     dtype = pieces[0].dtype
     out_shape = [jax.ShapeDtypeStruct((hours_dev, chunk_units * unit), dtype)] * groups
     out_specs = [piece_spec] * groups
+    if not has_next:
+        def body_index(i, place, *_):
+            turn = jnp.clip(i + lead - 2, 0, chunk_units - 2)
+            return 0, jnp.where(ascends(place[0]), turn, chunk_units - 2 - turn)
+
+        out_shape = out_shape[:-1] + [
+            jax.ShapeDtypeStruct((hours_dev, (chunk_units - 1) * unit), dtype),
+            jax.ShapeDtypeStruct((hours_dev, unit), dtype),
+        ]
+        out_specs = out_specs[:-1] + [
+            pl.BlockSpec((hours_dev, unit), body_index),
+            whole((hours_dev, unit)),
+        ]
     if has_next:
         out_shape += [jax.ShapeDtypeStruct((hours_all, 2 * unit), dtype)]
         out_specs += [whole((hours_all, 2 * unit))]
@@ -295,10 +317,10 @@
         ),
         name="products",
     )(place, neighbours, counts, *operands)
-    return results[:groups], (results[groups] if has_next else None)
-
-
-def place_kernel(peers, chunks, chunk, on_chip, *refs):
+    return results[:groups], results[groups]
+
+
+def place_kernel(peers, starts, unit, group_units, on_chip, *refs):
     target, sems = refs[-2], refs[-1]
     if on_chip:
         mine = lax.axis_index("tm")
@@ -310,7 +332,7 @@
         source = refs[which]
         columns = source.shape[1]
         group = place_ref[peer]
-        at = group * chunks + jnp.where(ascends(group), chunk, chunks - 1 - chunk)
+        at = (group * group_units + jnp.where(ascends(group), *starts)) * unit
         rows = source.shape[0] // ROW_COPIES
         for part in range(ROW_COPIES):
             copies.append(
@@ -318,7 +340,7 @@
                     source.at[part * rows : (part + 1) * rows],
                     target.at[
                         part * rows : (part + 1) * rows,
-                        pl.ds(pl.multiple_of(at * columns, columns), columns),
+                        pl.ds(pl.multiple_of(at, unit), columns),
                     ],
                     sems.at[which, part],
                 )
@@ -329,7 +351,7 @@
         copy.wait()
 
 
-def put(result, pieces, peers, place, cells_dev, chunks, chunk, on_chip):
+def put(result, pieces, peers, place, cells_dev, starts, unit, group_units, on_chip):
     hours_dev, columns = pieces[0].shape
     in_specs = [pl.BlockSpec(memory_space=pltpu.VMEM)] * len(pieces)
     operands = list(pieces)
@@ -342,7 +364,7 @@
         operands += [result]
         aliases = {len(scalars) + len(pieces): 0}
     return pl.pallas_call(
-        functools.partial(place_kernel, peers, chunks, chunk, on_chip),
+        functools.partial(place_kernel, peers, starts, unit, group_units, on_chip),
         out_shape=jax.ShapeDtypeStruct((hours_dev, cells_dev), pieces[0].dtype),
         grid_spec=pltpu.PrefetchScalarGridSpec(
             num_scalar_prefetch=len(scalars),
@@ -417,15 +439,20 @@
             spatial_blocks, layout, chunk,
         )
         returned.append(swap_all(outs))
+    final = swap(carry, groups - 1)
     for chunk in range(chunks):
         closing = chunk == chunks - 1
-        parts = [peers[:2], peers[2:-1], peers[-1:]] if closing else [peers]
-        for part, listed in enumerate(parts):
-            if listed:
-                result = put(
-                    result, [returned[chunk][peer] for peer in listed], listed, place,
-                    cells_dev, chunks, chunk, closing and part > 0,
-                )
+        up, down = chunk * chunk_units, group_units - (chunk + 1) * chunk_units
+        parts = [(peers, (up, down))]
+        if closing:
+            parts = [(peers[:2], (up, down)), (peers[2:-1], (up, down)), (peers[-1:], (up, down + 1))]
+        for part, (listed, starts) in enumerate(parts):
+            result = put(
+                result, [returned[chunk][peer] for peer in listed], listed, place,
+                cells_dev, starts, unit, group_units, closing and part > 0,
+            )
+    starts = (group_units - 1, 0)
+    result = put(result, [final], peers[-1:], place, cells_dev, starts, unit, group_units, True)
     return result
 
 

time: 312 us -> 306 us (0.981)
  waiting for transfers between devices: 200 us -> 184 us
  Pallas kernels: 87.1 us -> 96.9 us
    ppermute x18 -> x19, waiting for transfers between devices: 189 us -> 174 us  [swap(): return lax.ppermute(array, 'tm', [(at, at ^ peer) for at in range(groups)])]
    pallas_call x2, Pallas kernels: 53.6 us -> 62.7 us  [products(): pl.pallas_call(functools.partial(product_kernel, cfg), out_shape=out_shap...]
    ppermute x18 -> x19, starting transfers between devices: 10.4 us -> 12.2 us  [swap(): return lax.ppermute(array, 'tm', [(at, at ^ peer) for at in range(groups)])]
    pallas_call x4 -> x5, Pallas kernels: 12.9 us -> 13.5 us  [put(): pl.pallas_call(functools.partial(place_kernel, peers, starts, unit, group...]
  transfers between devices with their start and end apart: 20 -> 21, of which waited for: 10 -> 9; matrix products, arithmetic and copies ran while one was open for 0% -> 0% of each run, Pallas kernels for 26% -> 29%
where the time goes in v4:
time: 306 us; the launch traced here: 305 us
  waiting for transfers between devices  184 us (60%)
  Pallas kernels  96.9 us (32%)
  starting transfers between devices  18.1 us (6%)
  local copies, waits for them, and re-layouts  4.67 us (2%)
    ppermute x19, waiting for transfers between devices, swap(): return lax.ppermute(array, 'tm', [(at, at ^ peer) for at in range(groups)])  174 us
    pallas_call x2, Pallas kernels, products(): pl.pallas_call(functools.partial(product_kernel, cfg), out_shape=out_shap...  62.7 us
    pallas_call x5, Pallas kernels, put(): pl.pallas_call(functools.partial(place_kernel, peers, starts, unit, group...  13.5 us
    ppermute x19, starting transfers between devices, swap(): return lax.ppermute(array, 'tm', [(at, at ^ peer) for at in range(groups)])  12.2 us
    ppermute x1, waiting for transfers between devices, per_device(): high = lax.ppermute(field[:, :unit], 'space', backward)  10.2 us
    pallas_call x3, Pallas kernels, pack(): pl.pallas_call(functools.partial(copy_kernel, unit, sources, peers, on_ch...  8.16 us
    pallas_call x1, Pallas kernels, pack(): pl.pallas_call(functools.partial(pack_kernel, last, sources), out_shape=[...  7.87 us
  transfers between devices with their start and end apart: 21, of which 9 were waited for; matrix products, arithmetic and copies ran while one was open for 0% of the time, Pallas kernels for 29%

profile of v4, /device:TPU:16, one launch (start us, length us, event | category | flops | bytes accessed | tf_op | source)
XLA Modules:
  0.0 304.7 jit_solution(2225935392949529819)
XLA Ops:
  0.0 1.1 pack.4
  1.1 0.6 pad_add_fusion.place_ref.refs_0_
  1.7 5.9 %pack.5 = (bf16[256,3072]{1,0:T(8,128)(2,1)}, bf16[256,3072]{1,0:T(8,128)(2,1)}, bf16[256,3072]{1,0:T(8,128)(2,1)}, bf16[256,3072]{1,0:T(8,128)(2,1)}) custom-call(s32[5]{0:T(128)} %pad_add_fusion.place_ref.refs_0_, bf16[256,24576]{1,0:T(8,128)(2,1)} %refs_0_.5), custom_call_target="tpu_custom_call" | custom-call | bytes 12582912 | tf_op jit(solution)/shard_map/pack/pallas_call | solution.py:89
  7.6 0.1 collective-permute-start.5
  7.7 1.6 collective-permute-start.6
  9.3 0.3 collective-permute-start.7
  9.5 1.1 fusion
  10.6 3.3 %collective-permute-start.1 = (bf16[256,512]{1,0:T(8,128)(2,1)S(1)}, bf16[256,512]{1,0:T(8,128)(2,1)S(1)}, u32[]{:S(2)}, u32[]{:S(2)}) collective-permute-start(bf16[256,512]{1,0:T(8,128)(2,1)S(1)} %get-tuple-element.53), channel_id=1, source_target_pairs={{4,0},{8,4},{12,8},{16,12},{20,16},{24,20},{28,24},{5,1},{9,5},{13... | collective-permute-start | bytes 786440 | tf_op jit(solution)/shard_map/ppermute | solution.py:422
  13.9 2.6 collective-permute-start
  16.5 10.2 %collective-permute-done.1.refs_5_ = bf16[256,512]{1,0:T(8,128)(2,1)S(1)} collective-permute-done((bf16[256,512]{1,0:T(8,128)(2,1)S(1)}, bf16[256,512]{1,0:T(8,128)(2,1)S(1)}, u32[]{:S(2)}, u32[]{:S(2)}) %collective-permute-start.1) | collective-permute-done | bytes 262176 | tf_op jit(solution)/shard_map/ppermute | solution.py:422
  26.7 1.5 collective-permute-start.11
  28.2 0.0 collective-permute-done.refs_4_
  28.2 0.0 collective-permute-start.9
  28.2 1.2 pack.7
  29.4 55.1 %collective-permute-done.11.refs_10_ = bf16[256,512]{1,0:T(8,128)(2,1)S(1)} collective-permute-done((bf16[256,512]{1,0:T(8,128)(2,1)S(1)}, bf16[256,512]{1,0:T(8,128)(2,1)S(1)}, u32[]{:S(2)}, u32[]{:S(2)}) %collective-permute-start.11) | collective-permute-done | bytes 262176 | tf_op jit(solution)/shard_map/ppermute | solution.py:408
  84.6 4.5 %collective-permute-done.9.refs_11_ = bf16[256,512]{1,0:T(8,128)(2,1)S(1)} collective-permute-done((bf16[256,512]{1,0:T(8,128)(2,1)S(1)}, bf16[256,512]{1,0:T(8,128)(2,1)S(1)}, u32[]{:S(2)}, u32[]{:S(2)}) %collective-permute-start.9) | collective-permute-done | bytes 262176 | tf_op jit(solution)/shard_map/ppermute | solution.py:408
  89.1 0.4 collective-permute-start.8
  89.5 0.1 collective-permute-start.12
  89.6 1.0 collective-permute-done.8.refs_5_
  90.6 0.4 collective-permute-start.10
  91.0 7.9 %pack.6 = (bf16[256,3072]{1,0:T(8,128)(2,1)}, bf16[256,3072]{1,0:T(8,128)(2,1)}, bf16[256,3072]{1,0:T(8,128)(2,1)}, bf16[256,3072]{1,0:T(8,128)(2,1)}) custom-call(s32[5]{0:T(128)} %pad_add_fusion.place_ref.refs_0_, bf16[256,24576]{1,0:T(8,128)(2,1)} %refs_0_.5, bf16[256,24576]{1,0:T(8,128)(2,1)} %refs_0_.5, bf16[256,24576]{1,0:T(8,128)(2,1)} %refs_0_.5, ...), custom_call_target="tpu_custom_call" | custom-call | bytes 12582912 | tf_op jit(solution)/shard_map/pack/pallas_call | solution.py:108
  98.9 0.1 collective-permute-start.2
  99.0 0.0 collective-permute-done.10.refs_6_
  99.0 1.6 collective-permute-start.3
  100.6 0.2 collective-permute-start.4
  100.8 0.1 copy.11.neighbours_ref
  100.9 4.6 %order.1.cov_ref = bf16[1024,1024]{1,0:T(8,128)(2,1)} custom-call(s32[5]{0:T(128)} %pad_add_fusion.place_ref.refs_0_, bf16[1024,1024]{1,0:T(8,128)(2,1)} %source.1), custom_call_target="tpu_custom_call" | custom-call | tf_op jit(solution)/shard_map/order/pallas_call | solution.py:133
  105.5 0.0 collective-permute-done.6.refs_2_
  105.5 28.3 %products.2 = (bf16[256,3072]{1,0:T(8,128)(2,1)S(1)}, bf16[256,3072]{1,0:T(8,128)(2,1)S(1)}, bf16[256,3072]{1,0:T(8,128)(2,1)}, bf16[256,3072]{1,0:T(8,128)(2,1)}, bf16[1024,1024]{1,0:T(8,128)(2,1)}) custom-call(s32[5]{0:T(128)S(1)} %copy-done.2, s32[48,9]{1,0:T(8,128)S(1)} %copy.11.neighbours_ref, s32[48]{0:T(128)S(1)} %copy-done.3, ...), custom_call_target="tpu_custom_call" | custom-call | flops 16642998272 | bytes 21757952 | tf_op jit(solution)/shard_map/products/pallas_call | solution.py:297
  133.9 1.2 copy-done
  135.0 0.4 collective-permute-start.18
  135.4 1.6 collective-permute-start.19
  137.0 32.4 %collective-permute-done.4.refs_3_ = bf16[256,3072]{1,0:T(8,128)(2,1)} collective-permute-done((bf16[256,3072]{1,0:T(8,128)(2,1)}, bf16[256,3072]{1,0:T(8,128)(2,1)}, u32[]{:S(2)}, u32[]{:S(2)}) %collective-permute-start.4) | collective-permute-done | bytes 1572896 | tf_op jit(solution)/shard_map/ppermute | solution.py:408
  169.4 34.4 %products.3 = (bf16[256,3072]{1,0:T(8,128)(2,1)S(1)}, bf16[256,3072]{1,0:T(8,128)(2,1)}, bf16[256,3072]{1,0:T(8,128)(2,1)}, bf16[256,2560]{1,0:T(8,128)(2,1)}, bf16[256,512]{1,0:T(8,128)(2,1)S(1)}) custom-call(s32[5]{0:T(128)S(1)} %copy-done.2, s32[48,9]{1,0:T(8,128)S(1)} %copy.11.neighbours_ref, s32[48]{0:T(128)S(1)} %copy-done.3, ...), custom_call_target="tpu_custom_call" | custom-call | flops 14495514624 | bytes 19660800 | tf_op jit(solution)/shard_map/products/pallas_call | solution.py:297
  203.9 1.2 copy-done.1
  205.0 0.7 collective-permute-start.17
  205.7 1.6 collective-permute-start.16
  207.3 1.7 collective-permute-start.14
  209.1 27.8 %collective-permute-done.20.refs_4_ = bf16[256,3072]{1,0:T(8,128)(2,1)S(1)} collective-permute-done((bf16[256,3072]{1,0:T(8,128)(2,1)}, bf16[256,3072]{1,0:T(8,128)(2,1)S(1)}, u32[]{:S(2)}, u32[]{:S(2)}) %collective-permute-start.20) | collective-permute-done | bytes 1572896 | tf_op jit(solution)/shard_map/ppermute | solution.py:408
  236.8 1.1 copy-done.6
  238.0 6.3 %place.5.refs_3_ = bf16[256,24576]{1,0:T(8,128)(2,1)} custom-call(s32[5]{0:T(128)} %pad_add_fusion.place_ref.refs_0_, bf16[256,3072]{1,0:T(8,128)(2,1)} %copy-done, bf16[256,3072]{1,0:T(8,128)(2,1)} %copy-done.4, bf16[256,3072]{1,0:T(8,128)(2,1)} %copy-done.5, bf16[256,3072]{1,0:T(8,128)(2,1)} %copy-done.6), custom_call_target="tpu_custom_call" | custom-call | bytes 12582912 | tf_op jit(solution)/shard_map/place/pallas_call | solution.py:366
  244.3 4.3 %place.6.refs_1_ = bf16[256,24576]{1,0:T(8,128)(2,1)} custom-call(s32[5]{0:T(128)} %pad_add_fusion.place_ref.refs_0_, bf16[256,3072]{1,0:T(8,128)(2,1)} %copy-done.1, bf16[256,3072]{1,0:T(8,128)(2,1)} %collective-permute-done.17.refs_2_, bf16[256,24576]{1,0:T(8,128)(2,1)} %place.5.refs_3_), custom_call_target="tpu_custom_call", output_to_operand_aliasing={{}: (3, {})} | custom-call | bytes 6291456 | tf_op jit(solution)/shard_map/place/pallas_call | solution.py:366
  248.6 22.8 %collective-permute-done.16.refs_0_ = bf16[256,3072]{1,0:T(8,128)(2,1)S(1)} collective-permute-done((bf16[256,3072]{1,0:T(8,128)(2,1)}, bf16[256,3072]{1,0:T(8,128)(2,1)S(1)}, u32[]{:S(2)}, u32[]{:S(2)}) %collective-permute-start.16) | collective-permute-done | bytes 1572896 | tf_op jit(solution)/shard_map/ppermute | solution.py:408
  271.3 1.2 place.7.refs_1_
  272.5 26.1 %collective-permute-done.15.refs_0_ = bf16[256,2560]{1,0:T(8,128)(2,1)S(1)} collective-permute-done((bf16[256,2560]{1,0:T(8,128)(2,1)}, bf16[256,2560]{1,0:T(8,128)(2,1)S(1)}, u32[]{:S(2)}, u32[]{:S(2)}) %collective-permute-start.15) | collective-permute-done | bytes 1310752 | tf_op jit(solution)/shard_map/ppermute | solution.py:408
  298.6 1.1 place.8.refs_1_
  299.7 4.2 %collective-permute-done.14.refs_0_ = bf16[256,512]{1,0:T(8,128)(2,1)S(1)} collective-permute-done((bf16[256,512]{1,0:T(8,128)(2,1)S(1)}, bf16[256,512]{1,0:T(8,128)(2,1)S(1)}, u32[]{:S(2)}, u32[]{:S(2)}) %collective-permute-start.14) | collective-permute-done | bytes 262176 | tf_op jit(solution)/shard_map/ppermute | solution.py:408
  304.0 0.7 place.9
  (30 shorter events, 0.1 us)
Async XLA Ops:
  7.6 93.0 %collective-permute-start.5 = (bf16[256,3072]{1,0:T(8,128)(2,1)}, bf16[256,3072]{1,0:T(8,128)(2,1)}, u32[]{:S(2)}, u32[]{:S(2)}) collective-permute-start(bf16[256,3072]{1,0:T(8,128)(2,1)} %get-tuple-element.38), channel_id=1, source_target_pairs={{0,1},{1,0},{2,3},{3,2},{4,5},{5,4},{6,7},{7,6},{8,9},{9,8},{10,11... | collective-permute-start | bytes 4718600 | tf_op jit(solution)/shard_map/ppermute | solution.py:408
  7.7 97.8 %collective-permute-start.6 = (bf16[256,3072]{1,0:T(8,128)(2,1)}, bf16[256,3072]{1,0:T(8,128)(2,1)}, u32[]{:S(2)}, u32[]{:S(2)}) collective-permute-start(bf16[256,3072]{1,0:T(8,128)(2,1)} %get-tuple-element.39), channel_id=1, source_target_pairs={{0,2},{1,3},{2,0},{3,1},{4,6},{5,7},{6,4},{7,5},{8,10},{9,11},{10,... | collective-permute-start | bytes 4718600 | tf_op jit(solution)/shard_map/ppermute | solution.py:408
  9.3 96.2 %collective-permute-start.7 = (bf16[256,3072]{1,0:T(8,128)(2,1)}, bf16[256,3072]{1,0:T(8,128)(2,1)}, u32[]{:S(2)}, u32[]{:S(2)}) collective-permute-start(bf16[256,3072]{1,0:T(8,128)(2,1)} %get-tuple-element.31), channel_id=1, source_target_pairs={{0,3},{1,2},{2,1},{3,0},{4,7},{5,6},{6,5},{7,4},{8,11},{9,10},{10,... | collective-permute-start | bytes 4718600 | tf_op jit(solution)/shard_map/ppermute | solution.py:408
  10.6 16.1 %collective-permute-start.1 = (bf16[256,512]{1,0:T(8,128)(2,1)S(1)}, bf16[256,512]{1,0:T(8,128)(2,1)S(1)}, u32[]{:S(2)}, u32[]{:S(2)}) collective-permute-start(bf16[256,512]{1,0:T(8,128)(2,1)S(1)} %get-tuple-element.53), channel_id=1, source_target_pairs={{4,0},{8,4},{12,8},{16,12},{20,16},{24,20},{28,24},{5,1},{9,5},{13... | collective-permute-start | bytes 786440 | tf_op jit(solution)/shard_map/ppermute | solution.py:422
  13.9 14.3 %collective-permute-start = (bf16[256,512]{1,0:T(8,128)(2,1)S(1)}, bf16[256,512]{1,0:T(8,128)(2,1)S(1)}, u32[]{:S(2)}, u32[]{:S(2)}) collective-permute-start(bf16[256,512]{1,0:T(8,128)(2,1)S(1)} %get-tuple-element.54), channel_id=1, source_target_pairs={{0,4},{4,8},{8,12},{12,16},{16,20},{20,24},{24,28},{1,5},{5,9},{9,... | collective-permute-start | bytes 786440 | tf_op jit(solution)/shard_map/ppermute | solution.py:421
  26.7 2.7 copy-start.7
  26.7 57.9 %collective-permute-start.11 = (bf16[256,512]{1,0:T(8,128)(2,1)S(1)}, bf16[256,512]{1,0:T(8,128)(2,1)S(1)}, u32[]{:S(2)}, u32[]{:S(2)}) collective-permute-start(bf16[256,512]{1,0:T(8,128)(2,1)S(1)} %get-tuple-element.42), channel_id=1, source_target_pairs={{0,2},{1,3},{2,0},{3,1},{4,6},{5,7},{6,4},{7,5},{8,10},{9,11},{10,... | collective-permute-start | bytes 786440 | tf_op jit(solution)/shard_map/ppermute | solution.py:408
  28.2 1.2 copy-start.8
  28.2 60.9 %collective-permute-start.9 = (bf16[256,512]{1,0:T(8,128)(2,1)S(1)}, bf16[256,512]{1,0:T(8,128)(2,1)S(1)}, u32[]{:S(2)}, u32[]{:S(2)}) collective-permute-start(bf16[256,512]{1,0:T(8,128)(2,1)S(1)} %get-tuple-element.29), channel_id=1, source_target_pairs={{0,3},{1,2},{2,1},{3,0},{4,7},{5,6},{6,5},{7,4},{8,11},{9,10},{10,... | collective-permute-start | bytes 786440 | tf_op jit(solution)/shard_map/ppermute | solution.py:408
  84.6 4.9 %collective-permute-start.13 = (bf16[256,512]{1,0:T(8,128)(2,1)S(1)}, bf16[256,512]{1,0:T(8,128)(2,1)S(1)}, u32[]{:S(2)}, u32[]{:S(2)}) collective-permute-start(bf16[256,512]{1,0:T(8,128)(2,1)S(1)} %get-tuple-element.40.refs_4_), channel_id=1, source_target_pairs={{0,1},{1,0},{2,3},{3,2},{4,5},{5,4},{6,7},{7,6},{8,9},{9,8},{10,11... | collective-permute-start | bytes 786440 | tf_op jit(solution)/shard_map/ppermute | solution.py:408
  89.1 11.7 %copy-start.9 = (s32[48,9]{0,1:T(8,128)S(1)}, s32[48,9]{0,1:T(8,128)}, u32[]{:S(2)}) copy-start(s32[48,9]{0,1:T(8,128)} %param.8) | copy-start | bytes 5188
  89.1 1.5 collective-permute-start.8
  89.5 9.4 %collective-permute-start.12 = (bf16[256,512]{1,0:T(8,128)(2,1)S(1)}, bf16[256,512]{1,0:T(8,128)(2,1)S(1)}, u32[]{:S(2)}, u32[]{:S(2)}) collective-permute-start(bf16[256,512]{1,0:T(8,128)(2,1)S(1)} %collective-permute-done.11.refs_10_), channel_id=1, source_target_pairs={{0,1},{1,0},{2,3},{3,2},{4,5},{5,4},{6,7},{7,6},{8,9},{9,8},{10,11... | collective-permute-start | bytes 786440 | tf_op jit(solution)/shard_map/ppermute | solution.py:408
  90.6 8.4 %collective-permute-start.10 = (bf16[256,512]{1,0:T(8,128)(2,1)S(1)}, bf16[256,512]{1,0:T(8,128)(2,1)S(1)}, u32[]{:S(2)}, u32[]{:S(2)}) collective-permute-start(bf16[256,512]{1,0:T(8,128)(2,1)S(1)} %collective-permute-done.9.refs_11_), channel_id=1, source_target_pairs={{0,1},{1,0},{2,3},{3,2},{4,5},{5,4},{6,7},{7,6},{8,9},{9,8},{10,11... | collective-permute-start | bytes 786440 | tf_op jit(solution)/shard_map/ppermute | solution.py:408
  98.9 38.1 %collective-permute-start.2 = (bf16[256,3072]{1,0:T(8,128)(2,1)}, bf16[256,3072]{1,0:T(8,128)(2,1)}, u32[]{:S(2)}, u32[]{:S(2)}) collective-permute-start(bf16[256,3072]{1,0:T(8,128)(2,1)} %get-tuple-element.34), channel_id=1, source_target_pairs={{0,1},{1,0},{2,3},{3,2},{4,5},{5,4},{6,7},{7,6},{8,9},{9,8},{10,11... | collective-permute-start | bytes 4718600 | tf_op jit(solution)/shard_map/ppermute | solution.py:408
  99.0 38.0 %collective-permute-start.3 = (bf16[256,3072]{1,0:T(8,128)(2,1)}, bf16[256,3072]{1,0:T(8,128)(2,1)}, u32[]{:S(2)}, u32[]{:S(2)}) collective-permute-start(bf16[256,3072]{1,0:T(8,128)(2,1)} %get-tuple-element.35), channel_id=1, source_target_pairs={{0,2},{1,3},{2,0},{3,1},{4,6},{5,7},{6,4},{7,5},{8,10},{9,11},{10,... | collective-permute-start | bytes 4718600 | tf_op jit(solution)/shard_map/ppermute | solution.py:408
  100.6 68.8 %collective-permute-start.4 = (bf16[256,3072]{1,0:T(8,128)(2,1)}, bf16[256,3072]{1,0:T(8,128)(2,1)}, u32[]{:S(2)}, u32[]{:S(2)}) collective-permute-start(bf16[256,3072]{1,0:T(8,128)(2,1)} %get-tuple-element.36), channel_id=1, source_target_pairs={{0,3},{1,2},{2,1},{3,0},{4,7},{5,6},{6,5},{7,4},{8,11},{9,10},{10,... | collective-permute-start | bytes 4718600 | tf_op jit(solution)/shard_map/ppermute | solution.py:408
  100.9 4.6 %copy-start.2 = (s32[5]{0:T(128)S(1)}, s32[5]{0:T(128)}, u32[]{:S(2)}) copy-start(s32[5]{0:T(128)} %pad_add_fusion.place_ref.refs_0_) | copy-start | bytes 64
  100.9 4.6 %copy-start.3 = (s32[48]{0:T(128)S(1)}, s32[48]{0:T(128)}, u32[]{:S(2)}) copy-start(s32[48]{0:T(128)} %counts_ref.3) | copy-start | bytes 580
  133.8 1.2 copy-start
  135.0 72.3 %collective-permute-start.18 = (bf16[256,3072]{1,0:T(8,128)(2,1)S(1)}, bf16[256,3072]{1,0:T(8,128)(2,1)S(1)}, u32[]{:S(2)}, u32[]{:S(2)}) collective-permute-start(bf16[256,3072]{1,0:T(8,128)(2,1)S(1)} %get-tuple-element.50), channel_id=1, source_target_pairs={{0,1},{1,0},{2,3},{3,2},{4,5},{5,4},{6,7},{7,6},{8,9},{9,8},{10,11... | collective-permute-start | bytes 4718600 | tf_op jit(solution)/shard_map/ppermute | solution.py:408
  135.4 71.9 %collective-permute-start.19 = (bf16[256,3072]{1,0:T(8,128)(2,1)}, bf16[256,3072]{1,0:T(8,128)(2,1)S(1)}, u32[]{:S(2)}, u32[]{:S(2)}) collective-permute-start(bf16[256,3072]{1,0:T(8,128)(2,1)} %get-tuple-element.51), channel_id=1, source_target_pairs={{0,2},{1,3},{2,0},{3,1},{4,6},{5,7},{6,4},{7,5},{8,10},{9,11},{10,... | collective-permute-start | bytes 4718600 | tf_op jit(solution)/shard_map/ppermute | solution.py:408
  137.0 99.9 %collective-permute-start.20 = (bf16[256,3072]{1,0:T(8,128)(2,1)}, bf16[256,3072]{1,0:T(8,128)(2,1)S(1)}, u32[]{:S(2)}, u32[]{:S(2)}) collective-permute-start(bf16[256,3072]{1,0:T(8,128)(2,1)} %get-tuple-element.52), channel_id=1, source_target_pairs={{0,3},{1,2},{2,1},{3,0},{4,7},{5,6},{6,5},{7,4},{8,11},{9,10},{10,... | collective-permute-start | bytes 4718600 | tf_op jit(solution)/shard_map/ppermute | solution.py:408
  203.8 1.2 copy-start.1
  205.0 39.2 %collective-permute-start.17 = (bf16[256,3072]{1,0:T(8,128)(2,1)}, bf16[256,3072]{1,0:T(8,128)(2,1)}, u32[]{:S(2)}, u32[]{:S(2)}) collective-permute-start(bf16[256,3072]{1,0:T(8,128)(2,1)} %get-tuple-element.48), channel_id=1, source_target_pairs={{0,1},{1,0},{2,3},{3,2},{4,5},{5,4},{6,7},{7,6},{8,9},{9,8},{10,11... | collective-permute-start | bytes 4718600 | tf_op jit(solution)/shard_map/ppermute | solution.py:408
  205.7 65.6 %collective-permute-start.16 = (bf16[256,3072]{1,0:T(8,128)(2,1)}, bf16[256,3072]{1,0:T(8,128)(2,1)S(1)}, u32[]{:S(2)}, u32[]{:S(2)}) collective-permute-start(bf16[256,3072]{1,0:T(8,128)(2,1)} %get-tuple-element.46), channel_id=1, source_target_pairs={{0,2},{1,3},{2,0},{3,1},{4,6},{5,7},{6,4},{7,5},{8,10},{9,11},{10,... | collective-permute-start | bytes 4718600 | tf_op jit(solution)/shard_map/ppermute | solution.py:408
  207.3 1.8 copy-start.4
  207.3 91.3 %collective-permute-start.15 = (bf16[256,2560]{1,0:T(8,128)(2,1)}, bf16[256,2560]{1,0:T(8,128)(2,1)S(1)}, u32[]{:S(2)}, u32[]{:S(2)}) collective-permute-start(bf16[256,2560]{1,0:T(8,128)(2,1)} %get-tuple-element.45), channel_id=1, source_target_pairs={{0,3},{1,2},{2,1},{3,0},{4,7},{5,6},{6,5},{7,4},{8,11},{9,10},{10,... | collective-permute-start | bytes 3932168 | tf_op jit(solution)/shard_map/ppermute | solution.py:408
  207.3 29.5 %copy-start.5 = (bf16[256,3072]{1,0:T(8,128)(2,1)}, bf16[256,3072]{1,0:T(8,128)(2,1)S(1)}, u32[]{:S(2)}) copy-start(bf16[256,3072]{1,0:T(8,128)(2,1)S(1)} %collective-permute-done.19.refs_3_) | copy-start | bytes 4718596
  207.3 96.6 %collective-permute-start.14 = (bf16[256,512]{1,0:T(8,128)(2,1)S(1)}, bf16[256,512]{1,0:T(8,128)(2,1)S(1)}, u32[]{:S(2)}, u32[]{:S(2)}) collective-permute-start(bf16[256,512]{1,0:T(8,128)(2,1)S(1)} %get-tuple-element.44), channel_id=1, source_target_pairs={{0,3},{1,2},{2,1},{3,0},{4,7},{5,6},{6,5},{7,4},{8,11},{9,10},{10,... | collective-permute-start | bytes 786440 | tf_op jit(solution)/shard_map/ppermute | solution.py:408
  236.8 1.1 copy-start.6
